TPU v7x, 256 devices: a whole 4x4x8 slice. The times are simulated.
256 devices in a mesh: dom: 64 (over y, z, core), mat: 4 (over x).
Axes of the slice: x: 4, y: 4, z: 8, core: 2. Of those that a mesh axis runs over, the one named last changes fastest.
Arguments:
- orbitals: bfloat16 [16384, 12, 32, 128], P('dom', None, 'mat')
- potential: float32 [256, 32, 128], P('dom', 'mat'), may hold values from -3 to 3
- centre_first: int32 [16384], P('dom'), may hold values from 0 to 3
- centre_second: int32 [16384], P('dom'), may hold values from 0 to 31
- centre_third: int32 [16384], P('dom'), may hold values from 0 to 127
- correlation_pairs: int32 [128, 5, 2], P('dom'), may hold values from 0 to 1, as said below
Outputs:
- gram_rows: float32 [5, 256, 16384], P(None, 'mat', 'dom')
- hamiltonian_rows: float32 [5, 256, 16384], P(None, 'mat', 'dom')
Inputs may be any that keep to these rules, and one draw needn't show every extreme that they name: correlation_pairs[g, k, b] refers to block b of the domain k - 2 away from block g's owner (wrapping); the pattern is symmetric between the two blocks, and every pair of blocks of one domain is 1.
All inputs are finite; a program needn't handle non-finite values.
Results may differ from a plain program's by a relative error of at most 0.00043.
Values may be sent and summed in bfloat16 or wider, within the bound.
A program may use at most 128 MiB of HBM per device.

v0:
```python
import jax
import jax.numpy as jnp
from jax import lax
from jax.sharding import PartitionSpec as P


def extended_2(array, sides, width):
    for axis, dim in sides:
        size, length = (lax.axis_size(axis), array.shape[dim])
        up = [(i, (i + 1) % size) for i in range(size)]
        down = [(j, i) for i, j in up]
        last = lax.slice_in_dim(array, length - width, length, axis=dim)
        first = lax.slice_in_dim(array, 0, width, axis=dim)
        before = lax.ppermute(last, axis, up)
        after = lax.ppermute(first, axis, down)
        array = jnp.concatenate([before, array, after], axis=dim)
    return array


def passed_along(block, axis, distance):
    devices = range(lax.axis_size(axis))
    route = [((i - distance) % len(devices), i) for i in devices]
    return lax.ppermute(block, axis, route)


def sphere_mask(
    centre_first,
    centre_second,
    centre_third,
    window_cells,
    patch_cells,
    second_cells,
    second_start,
    second_total,
    third_cells,
):
    planes = lax.iota(jnp.int32, window_cells)
    off_first = planes[None, :] - (patch_cells + centre_first[:, None])
    interior = (planes >= 1) & (planes <= window_cells - 2)
    second_coord = second_start + lax.iota(jnp.int32, second_cells)
    off_second = jnp.mod(second_coord[None, :] - centre_second[:, None], second_total)
    off_second = jnp.minimum(off_second, second_total - off_second)
    off_third = lax.iota(jnp.int32, third_cells)[None, :] - centre_third[:, None]
    radius = window_cells // 2
    distance = (
        (off_first * off_first)[:, :, None, None]
        + (off_second * off_second)[:, None, :, None]
        + (off_third * off_third)[:, None, None, :]
    )
    return (distance <= radius * radius) & interior[None, :, None, None]


def stencil(extended, potential_slab):
    centre_cells = extended[:, 1:-1, 1:-1, :].astype(jnp.float32)
    beside = extended[:, 2:, 1:-1, :].astype(jnp.float32) + extended[:, :-2, 1:-1, :].astype(
        jnp.float32
    )
    beside = (
        beside
        + extended[:, 1:-1, 2:, :].astype(jnp.float32)
        + extended[:, 1:-1, :-2, :].astype(jnp.float32)
    )
    third_padded = jnp.pad(centre_cells, ((0, 0), (0, 0), (0, 0), (1, 1)))
    beside = beside + third_padded[..., 2:] + third_padded[..., :-2]
    return 0.5 * (6.0 * centre_cells - beside) + potential_slab[None] * centre_cells


def on_device(orbitals, potential, centre_first, centre_second, centre_third, correlation_pairs):
    block_orbs, window_cells, second_cells, third_cells = orbitals.shape
    patch_cells = potential.shape[0]
    local_blocks = correlation_pairs.shape[0]
    per_block = block_orbs // local_blocks
    mat_count = lax.axis_size("mat")
    second_start = lax.axis_index("mat") * second_cells
    inside = sphere_mask(
        centre_first,
        centre_second,
        centre_third,
        window_cells,
        patch_cells,
        second_cells,
        second_start,
        second_cells * mat_count,
        third_cells,
    )
    masked = jnp.where(inside, orbitals, jnp.zeros_like(orbitals))
    upper_start = 2 * patch_cells
    rimmed = extended_2(masked, (("mat", 2),), 1)
    rimmed = jnp.pad(rimmed, ((0, 0), (1, 1), (0, 0), (0, 0)))
    potential_window = extended_2(potential, (("dom", 0),), patch_cells)
    applied = stencil(rimmed, potential_window).astype(jnp.bfloat16)
    paired = jnp.stack([masked, applied])
    received = []
    for offset, low_plane in ((1, upper_start), (-1, 0)):
        sent_piece = paired[:, :, low_plane : low_plane + patch_cells]
        received.append(passed_along(sent_piece, "dom", offset))
    middle = paired[:, :, patch_cells:upper_start]
    slot_stack = jnp.concatenate([received[0], middle, received[1]], axis=1)
    orbital_block = slot_stack[0].reshape(3 * block_orbs, -1)
    applied_block = slot_stack[1].reshape(3 * block_orbs, -1)
    gram_full = lax.dot_general(
        orbital_block, orbital_block, (((1,), (1,)), ((), ())), preferred_element_type=jnp.float32
    )
    energy_full = lax.dot_general(
        applied_block, orbital_block, (((1,), (1,)), ((), ())), preferred_element_type=jnp.float32
    )
    gram_full = gram_full.reshape(3, block_orbs, 3, block_orbs)
    energy_full = energy_full.reshape(3, block_orbs, 3, block_orbs)
    gram_part, energy_part = (
        lax.psum_scatter(gram_full, "mat", scatter_dimension=1, tiled=True),
        lax.psum_scatter(energy_full, "mat", scatter_dimension=1, tiled=True),
    )
    col_count = block_orbs // mat_count
    strips = jnp.stack([gram_part, energy_part])
    assembled = jnp.pad(strips[:, :, :, 1], ((0, 0), (1, 1), (0, 0), (0, 0)))
    for slot_index, offset in ((0, -1), (2, 1)):
        arrived = passed_along(strips[:, :, :, slot_index], "dom", offset)
        assembled = assembled + jnp.pad(
            arrived, ((0, 0), (2 - slot_index, slot_index), (0, 0), (0, 0))
        )
    columns = lax.axis_index("mat") * col_count + lax.iota(jnp.int32, col_count)
    block_ids = lax.iota(jnp.int32, local_blocks)
    column_pick = ((columns // per_block)[:, None] == block_ids[None, :]).astype(jnp.float32)
    row_pick = (
        (lax.iota(jnp.int32, block_orbs) // per_block)[:, None] == block_ids[None, :]
    ).astype(jnp.float32)
    select = jnp.einsum(
        "rkb,cb,ar->kca", correlation_pairs.astype(jnp.float32), column_pick, row_pick
    )
    return (assembled[0] * select, assembled[1] * select)


def solution(mesh):
    return jax.shard_map(
        on_device,
        mesh=mesh,
        in_specs=(
            P("dom", None, "mat", None),
            P("dom", "mat", None),
            P("dom"),
            P("dom"),
            P("dom"),
            P("dom", None, None),
        ),
        out_specs=(P(None, "mat", "dom"), P(None, "mat", "dom")),
        check_vma=False,
    )
```

profile of v0, /device:TPU:6, one launch (start us, length us, event | category | flops | bytes accessed | tf_op | source)
XLA Modules:
  0.0 274.3 jit_solution(4575311594283140444)
XLA Ops:
  9.5 8.1 %fusion.40 = (f32[256,12,8,128]{3,0,2,1:T(8,128)}, bf16[256,12,8,128]{3,0,2,1:T(8,128)(2,1)S(1)}) fusion(bf16[256,12,8,128]{3,2,1,0:T(8,128)(2,1)} %param.6, pred[12]{0:T(512)(128)(4,1)S(1)} %compare_and_fusion, s32[256,128]{1,0:T(8,128)S(1)} %subtract_multiply_fusion, s32[256,12,8]{0,2,1:T(8,128)S(1)} %broadcast_add_fusion), kind=kLoop, calls=%fused_computation.83 | loop fusion | flops 15728640 | bytes 25395212 | tf_op jit(solution)/shard_map/convert_element_type | solution.py:54
  17.7 2.3 collective-permute-start
  20.1 7.0 %collective-permute-start.3 = (f32[4,8,128]{2,1,0:T(8,128)S(1)}, f32[4,8,128]{2,1,0:T(8,128)S(1)}, u32[]{:S(2)}, u32[]{:S(2)}) collective-permute-start(f32[4,8,128]{2,1,0:T(8,128)S(1)} %copy-done), channel_id=1, source_target_pairs={{4,0},{8,4},{12,8},{16,12},{20,16},{24,20},{28,24},{32,28},{36,32}... | collective-permute-start | bytes 49160 | tf_op jit(solution)/shard_map/ppermute | solution.py:15
  27.0 1.4 collective-permute-done.2
  28.5 8.6 %collective-permute-done = bf16[256,12,1,128]{3,0,2,1:T(8,128)(2,1)S(1)} collective-permute-done((bf16[256,12,1,128]{3,0,2,1:T(8,128)(2,1)S(1)}, bf16[256,12,1,128]{3,0,2,1:T(8,128)(2,1)S(1)}, u32[]{:S(2)}, u32[]{:S(2)}) %collective-permute-start) | collective-permute-done | bytes 786464 | tf_op jit(solution)/shard_map/ppermute | solution.py:14
  38.4 3.2 %fusion.15 = bf16[256,14,10,128]{3,0,2,1:T(8,128)(2,1)S(1)} fusion(bf16[256,12,1,128]{3,0,2,1:T(8,128)(2,1)S(1)} %collective-permute-done.1, bf16[256,12,8,128]{3,0,2,1:T(8,128)(2,1)S(1)} %get-tuple-element.3, bf16[256,12,1,128]{3,0,2,1:T(8,128)(2,1)S(1)} %collective-permute-done), kind=kLoop, calls=%fused_computation.25 | loop fusion | flops 55050240 | bytes 17039360 | tf_op jit(solution)/shard_map/concatenate | solution.py:16
  41.6 21.0 %fusion.18 = bf16[1,256,12,8,128]{4,1,3,2,0:T(8,128)(2,1)} fusion(f32[256,12,8,128]{3,0,2,1:T(8,128)} %get-tuple-element.2, f32[12,8,128]{2,1,0:T(8,128)S(1)} %pad_maximum_fusion.5, bf16[256,12,8,128]{3,0,2,1:T(8,128)(2,1)S(1)} %get-tuple-element.3, bf16[256,12,1,128]{3,0,2,1:T(8,128)(2,1)S(1)} %collective-permute-done, ...), kind=kLoop, calls=%fused_computation.30 | loop fusion | flops 53477376 | bytes 39370752 | tf_op jit(solution)/shard_map/stack | solution.py:92
  62.6 4.1 %fusion.20 = (bf16[2,256,4,8,128]{4,1,3,2,0:T(8,128)(2,1)S(1)}, bf16[2,256,4,8,128]{4,1,3,2,0:T(8,128)(2,1)S(1)}, bf16[2,256,4,8,128]{4,1,3,2,0:T(8,128)(2,1)S(1)}) fusion(bf16[1,256,12,8,128]{4,1,3,2,0:T(8,128)(2,1)S(1)} %bitcast.45, bf16[1,256,12,8,128]{4,1,3,2,0:T(8,128)(2,1)} %fusion.18), kind=kLoop, calls=%fused_computation.32 | loop fusion | flops 6291456 | bytes 25165824 | tf_op jit(solution)/shard_map/stack | solution.py:92
  66.8 6.9 %collective-permute-start.5 = (bf16[2,256,4,8,128]{4,1,3,2,0:T(8,128)(2,1)S(1)}, bf16[2,256,4,8,128]{4,1,3,2,0:T(8,128)(2,1)S(1)}, u32[]{:S(2)}, u32[]{:S(2)}) collective-permute-start(bf16[2,256,4,8,128]{4,1,3,2,0:T(8,128)(2,1)S(1)} %get-tuple-element.7), channel_id=1, source_target_pairs={{4,0},{8,4},{12,8},{16,12},{20,16},{24,20},{28,24},{32,28},{36,32}... | collective-permute-start | bytes 12582920 | tf_op jit(solution)/shard_map/ppermute | solution.py:23
  73.7 45.9 %collective-permute-done.4 = bf16[2,256,4,8,128]{4,1,3,2,0:T(8,128)(2,1)S(1)} collective-permute-done((bf16[2,256,4,8,128]{4,1,3,2,0:T(8,128)(2,1)S(1)}, bf16[2,256,4,8,128]{4,1,3,2,0:T(8,128)(2,1)S(1)}, u32[]{:S(2)}, u32[]{:S(2)}) %collective-permute-start.4) | collective-permute-done | bytes 4194336 | tf_op jit(solution)/shard_map/ppermute | solution.py:23
  119.7 9.9 %pad_maximum_fusion = bf16[2,768,4,8,128]{4,1,3,2,0:T(8,128)(2,1)S(1)} fusion(bf16[2,256,4,8,128]{4,1,3,2,0:T(8,128)(2,1)S(1)} %collective-permute-done.5, bf16[2,256,4,8,128]{4,1,3,2,0:T(8,128)(2,1)S(1)} %get-tuple-element.8, bf16[2,256,4,8,128]{4,1,3,2,0:T(8,128)(2,1)S(1)} %collective-permute-done.4), kind=kLoop, calls=%fused_computation.15 | loop fusion | flops 37748736 | bytes 25165824 | tf_op jit(solution)/shard_map/concatenate | solution.py:98
  129.6 4.2 %fusion.42 = (bf16[1,768,4,8,128]{4,1,3,2,0:T(8,128)(2,1)}, bf16[1,768,4,8,128]{4,1,3,2,0:T(8,128)(2,1)S(1)}) fusion(bf16[2,768,4,8,128]{4,1,3,2,0:T(8,128)(2,1)S(1)} %pad_maximum_fusion), kind=kLoop, calls=%fused_computation.84 | loop fusion | bytes 25165824 | tf_op jit(solution)/shard_map/slice | solution.py:100
  133.8 6.6 %copy.11 = bf16[1,768,4,8,128]{4,3,2,1,0:T(8,128)(2,1)} copy(bf16[1,768,4,8,128]{4,1,3,2,0:T(8,128)(2,1)S(1)} %get-tuple-element.5) | data formatting | bytes 12582912 | tf_op jit(solution)/shard_map/slice | solution.py:99
  140.5 10.3 %reshape.145 = bf16[3,256,4096,1]{2,1,0,3:T(8,128)(2,1)} reshape(bf16[1,768,4,8,128]{4,3,2,1,0:T(8,128)(2,1)} %copy.11) | data formatting | bytes 12582912 | tf_op jit(solution)/shard_map/dot_general | solution.py:101
  150.8 9.4 %copy.12 = bf16[1,768,4,8,128]{4,3,2,1,0:T(8,128)(2,1)} copy(bf16[1,768,4,8,128]{4,1,3,2,0:T(8,128)(2,1)} %get-tuple-element.4) | data formatting | bytes 12582912 | tf_op jit(solution)/shard_map/slice | solution.py:100
  160.2 10.3 %reshape.146 = bf16[3,256,4096,1]{2,1,0,3:T(8,128)(2,1)} reshape(bf16[1,768,4,8,128]{4,3,2,1,0:T(8,128)(2,1)} %copy.12) | data formatting | bytes 12582912 | tf_op jit(solution)/shard_map/dot_general | solution.py:104
  170.5 10.1 %fusion.16 = f32[3,256,3,256]{3,1,2,0:T(8,128)} fusion(bf16[3,256,4096,1]{2,1,0,3:T(8,128)(2,1)} %reshape.145, bf16[3,256,4096,1]{2,1,0,3:T(8,128)(2,1)} %reshape.146), kind=kOutput, calls=%fused_computation.28 | convolution fusion | flops 4831838208 | bytes 14942208 | tf_op jit(solution)/shard_map/dot_general | solution.py:104
  180.7 10.1 %fusion.12 = f32[3,256,3,256]{3,1,2,0:T(8,128)} fusion(bf16[3,256,4096,1]{2,1,0,3:T(8,128)(2,1)} %reshape.145), kind=kOutput, calls=%fused_computation.22 | convolution fusion | flops 4831838208 | bytes 8650752 | tf_op jit(solution)/shard_map/dot_general | solution.py:101
  190.8 21.7 %reduce-scatter.5.cloned.1.call-done = f32[3,64,3,256]{3,1,2,0:T(8,128)} async-done(((f32[3,256,3,256]{3,1,2,0:T(8,128)}), f32[3,64,3,256]{3,1,2,0:T(8,128)}) %reduce-scatter.5.cloned.1.call-update) | async-done | bytes 589840 | tf_op jit(solution)/shard_map/reduce_scatter | solution.py:111
  212.5 36.7 %reduce-scatter.3.cloned.1.call-done = f32[3,64,3,256]{3,1,2,0:T(8,128)} async-done(((f32[3,256,3,256]{3,1,2,0:T(8,128)}), f32[3,64,3,256]{3,1,2,0:T(8,128)}) %reduce-scatter.3.cloned.1.call-update) | async-done | bytes 589840 | tf_op jit(solution)/shard_map/reduce_scatter | solution.py:110
  249.2 1.4 fusion.24
  250.7 5.1 %collective-permute-start.6 = (f32[2,3,64,256]{3,2,1,0:T(8,128)S(1)}, f32[2,3,64,256]{3,2,1,0:T(8,128)S(1)}, u32[]{:S(2)}, u32[]{:S(2)}) collective-permute-start(f32[2,3,64,256]{3,2,1,0:T(8,128)S(1)} %get-tuple-element.13), channel_id=1, source_target_pairs={{4,0},{8,4},{12,8},{16,12},{20,16},{24,20},{28,24},{32,28},{36,32}... | collective-permute-start | bytes 1179656 | tf_op jit(solution)/shard_map/ppermute | solution.py:23
  256.0 5.1 %collective-permute-done.6 = f32[2,3,64,256]{3,2,1,0:T(8,128)S(1)} collective-permute-done((f32[2,3,64,256]{3,2,1,0:T(8,128)S(1)}, f32[2,3,64,256]{3,2,1,0:T(8,128)S(1)}, u32[]{:S(2)}, u32[]{:S(2)}) %collective-permute-start.6) | collective-permute-done | bytes 393248 | tf_op jit(solution)/shard_map/ppermute | solution.py:23
  261.0 5.2 %collective-permute-done.7 = f32[2,3,64,256]{3,2,1,0:T(8,128)S(1)} collective-permute-done((f32[2,3,64,256]{3,2,1,0:T(8,128)S(1)}, f32[2,3,64,256]{3,2,1,0:T(8,128)S(1)}, u32[]{:S(2)}, u32[]{:S(2)}) %collective-permute-start.7) | collective-permute-done | bytes 393248 | tf_op jit(solution)/shard_map/ppermute | solution.py:23
  (29 shorter events, 5.4 us)
Async XLA Ops:
  7.2 205.4 %reduce-scatter.5.cloned.1.call-start = ((), (), s32[]{:S(2)}) async-start(), calls=%async_computation.3 | async-start | bytes 2949120 | tf_op jit(solution)/shard_map/reduce_scatter | solution.py:111
  9.5 10.6 %copy-start = (f32[4,8,128]{2,1,0:T(8,128)S(1)}, f32[4,8,128]{2,1,0:T(8,128)}, u32[]{:S(2)}) copy-start(f32[4,8,128]{2,1,0:T(8,128)} %param.7) | copy-start | bytes 49156
  17.7 19.4 %collective-permute-start = (bf16[256,12,1,128]{3,0,2,1:T(8,128)(2,1)S(1)}, bf16[256,12,1,128]{3,0,2,1:T(8,128)(2,1)S(1)}, u32[]{:S(2)}, u32[]{:S(2)}) collective-permute-start(bf16[256,12,1,128]{3,0,2,1:T(8,128)(2,1)S(1)} %get-tuple-element.10), channel_id=1, source_target_pairs={{0,1},{1,2},{2,3},{3,0},{4,5},{5,6},{6,7},{7,4},{8,9},{9,10},{10,1... | collective-permute-start | bytes 2359304 | tf_op jit(solution)/shard_map/ppermute | solution.py:14
  20.0 18.4 %collective-permute-start.1 = (bf16[256,12,1,128]{3,0,2,1:T(8,128)(2,1)S(1)}, bf16[256,12,1,128]{3,0,2,1:T(8,128)(2,1)S(1)}, u32[]{:S(2)}, u32[]{:S(2)}) collective-permute-start(bf16[256,12,1,128]{3,0,2,1:T(8,128)(2,1)S(1)} %get-tuple-element.9), channel_id=1, source_target_pairs={{1,0},{2,1},{3,2},{0,3},{5,4},{6,5},{7,6},{4,7},{9,8},{10,9},{11,1... | collective-permute-start | bytes 2359304 | tf_op jit(solution)/shard_map/ppermute | solution.py:15
  20.0 8.4 %collective-permute-start.2 = (f32[4,8,128]{2,1,0:T(8,128)S(1)}, f32[4,8,128]{2,1,0:T(8,128)S(1)}, u32[]{:S(2)}, u32[]{:S(2)}) collective-permute-start(f32[4,8,128]{2,1,0:T(8,128)S(1)} %copy-done), channel_id=1, source_target_pairs={{0,4},{4,8},{8,12},{12,16},{16,20},{20,24},{24,28},{28,32},{32,36}... | collective-permute-start | bytes 49160 | tf_op jit(solution)/shard_map/ppermute | solution.py:14
  20.1 8.4 %collective-permute-start.3 = (f32[4,8,128]{2,1,0:T(8,128)S(1)}, f32[4,8,128]{2,1,0:T(8,128)S(1)}, u32[]{:S(2)}, u32[]{:S(2)}) collective-permute-start(f32[4,8,128]{2,1,0:T(8,128)S(1)} %copy-done), channel_id=1, source_target_pairs={{4,0},{8,4},{12,8},{16,12},{20,16},{24,20},{28,24},{32,28},{36,32}... | collective-permute-start | bytes 49160 | tf_op jit(solution)/shard_map/ppermute | solution.py:15
  66.7 52.9 %collective-permute-start.4 = (bf16[2,256,4,8,128]{4,1,3,2,0:T(8,128)(2,1)S(1)}, bf16[2,256,4,8,128]{4,1,3,2,0:T(8,128)(2,1)S(1)}, u32[]{:S(2)}, u32[]{:S(2)}) collective-permute-start(bf16[2,256,4,8,128]{4,1,3,2,0:T(8,128)(2,1)S(1)} %get-tuple-element.6), channel_id=1, source_target_pairs={{252,0},{0,4},{4,8},{8,12},{12,16},{16,20},{20,24},{24,28},{28,32}... | collective-permute-start | bytes 12582920 | tf_op jit(solution)/shard_map/ppermute | solution.py:23
  66.8 52.9 %collective-permute-start.5 = (bf16[2,256,4,8,128]{4,1,3,2,0:T(8,128)(2,1)S(1)}, bf16[2,256,4,8,128]{4,1,3,2,0:T(8,128)(2,1)S(1)}, u32[]{:S(2)}, u32[]{:S(2)}) collective-permute-start(bf16[2,256,4,8,128]{4,1,3,2,0:T(8,128)(2,1)S(1)} %get-tuple-element.7), channel_id=1, source_target_pairs={{4,0},{8,4},{12,8},{16,12},{20,16},{24,20},{28,24},{32,28},{36,32}... | collective-permute-start | bytes 12582920 | tf_op jit(solution)/shard_map/ppermute | solution.py:23
  180.6 75.2 %copy-start.1 = (s32[2,5,2]{1,2,0:T(2,128)S(1)}, s32[2,5,2]{1,2,0:T(2,128)}, u32[]{:S(2)}) copy-start(s32[2,5,2]{1,2,0:T(2,128)} %param.11) | copy-start | bytes 244
  180.6 68.6 %reduce-scatter.3.cloned.1.call-start = ((), (), s32[]{:S(2)}) async-start(), calls=%async_computation.2 | async-start | bytes 2949120 | tf_op jit(solution)/shard_map/reduce_scatter | solution.py:110
  250.7 10.4 %collective-permute-start.6 = (f32[2,3,64,256]{3,2,1,0:T(8,128)S(1)}, f32[2,3,64,256]{3,2,1,0:T(8,128)S(1)}, u32[]{:S(2)}, u32[]{:S(2)}) collective-permute-start(f32[2,3,64,256]{3,2,1,0:T(8,128)S(1)} %get-tuple-element.13), channel_id=1, source_target_pairs={{4,0},{8,4},{12,8},{16,12},{20,16},{24,20},{28,24},{32,28},{36,32}... | collective-permute-start | bytes 1179656 | tf_op jit(solution)/shard_map/ppermute | solution.py:23
  255.7 10.5 %collective-permute-start.7 = (f32[2,3,64,256]{3,2,1,0:T(8,128)S(1)}, f32[2,3,64,256]{3,2,1,0:T(8,128)S(1)}, u32[]{:S(2)}, u32[]{:S(2)}) collective-permute-start(f32[2,3,64,256]{3,2,1,0:T(8,128)S(1)} %get-tuple-element.12), channel_id=1, source_target_pairs={{252,0},{0,4},{4,8},{8,12},{12,16},{16,20},{20,24},{24,28},{28,32}... | collective-permute-start | bytes 1179656 | tf_op jit(solution)/shard_map/ppermute | solution.py:23
Sparse Core Ops, SparseCore 0:
  180.7 31.7 reduce-scatter.4
  215.1 34.0 reduce-scatter.2
where the time goes:
time: 276 us; the launch traced here: 274 us
  waiting for transfers between devices  126 us (46%)
  other arithmetic  50 us (18%)
  local copies, waits for them, and re-layouts  41.1 us (15%)
  starting transfers between devices  21.5 us (8%)
  matrix products  21.5 us (8%)
  between operations  14.2 us (5%)
    ppermute x4, waiting for transfers between devices, passed_along(): return lax.ppermute(block, axis, route)  56.3 us
    reduce_scatter x1, waiting for transfers between devices, on_device(): lax.psum_scatter(gram_full, 'mat', scatter_dimension=1, tiled=True)  36.7 us
    another operation x2, other arithmetic, on_device(): paired = jnp.stack([masked, applied])  25.1 us
    reduce_scatter x1, waiting for transfers between devices, on_device(): lax.psum_scatter(energy_full, 'mat', scatter_dimension=1, tiled=True)  21.7 us
    slice x2, local copies, waits for them, and re-layouts, on_device(): applied_block = slot_stack[1].reshape(3 * block_orbs, -1)  13.7 us
    ppermute x4, starting transfers between devices, passed_along(): return lax.ppermute(block, axis, route)  12.1 us
    dot_general x1, local copies, waits for them, and re-layouts, on_device(): lax.dot_general(orbital_block, orbital_block, (((1,), (1,)), ((), ())), p...  10.3 us
    dot_general x1, local copies, waits for them, and re-layouts, on_device(): lax.dot_general(applied_block, orbital_block, (((1,), (1,)), ((), ())), p...  10.3 us
  transfers between devices with their start and end apart: 10, of which 9 were waited for; matrix products, arithmetic and copies ran while one was open for 4% of the time, Pallas kernels for 0%

commit v1 on v0

--- a/solution.py
+++ b/solution.py
@@ -65,6 +65,12 @@
     return 0.5 * (6.0 * centre_cells - beside) + potential_slab[None] * centre_cells
 
 
+def pair_product(left, right):
+    return lax.dot_general(
+        left, right, (((1, 2, 3), (1, 2, 3)), ((), ())), preferred_element_type=jnp.float32
+    )
+
+
 def on_device(orbitals, potential, centre_first, centre_second, centre_third, correlation_pairs):
     block_orbs, window_cells, second_cells, third_cells = orbitals.shape
     patch_cells = potential.shape[0]
@@ -85,31 +91,31 @@
     )
     masked = jnp.where(inside, orbitals, jnp.zeros_like(orbitals))
     upper_start = 2 * patch_cells
+    phi_slots = [
+        passed_along(masked[:, upper_start:], "dom", 1),
+        masked[:, patch_cells:upper_start],
+        passed_along(masked[:, :patch_cells], "dom", -1),
+    ]
     rimmed = extended_2(masked, (("mat", 2),), 1)
     rimmed = jnp.pad(rimmed, ((0, 0), (1, 1), (0, 0), (0, 0)))
     potential_window = extended_2(potential, (("dom", 0),), patch_cells)
     applied = stencil(rimmed, potential_window).astype(jnp.bfloat16)
-    paired = jnp.stack([masked, applied])
-    received = []
-    for offset, low_plane in ((1, upper_start), (-1, 0)):
-        sent_piece = paired[:, :, low_plane : low_plane + patch_cells]
-        received.append(passed_along(sent_piece, "dom", offset))
-    middle = paired[:, :, patch_cells:upper_start]
-    slot_stack = jnp.concatenate([received[0], middle, received[1]], axis=1)
-    orbital_block = slot_stack[0].reshape(3 * block_orbs, -1)
-    applied_block = slot_stack[1].reshape(3 * block_orbs, -1)
-    gram_full = lax.dot_general(
-        orbital_block, orbital_block, (((1,), (1,)), ((), ())), preferred_element_type=jnp.float32
+    applied_slots = [
+        passed_along(applied[:, upper_start:], "dom", 1),
+        applied[:, patch_cells:upper_start],
+        passed_along(applied[:, :patch_cells], "dom", -1),
+    ]
+    gram_full = jnp.stack(
+        [jnp.stack([pair_product(phi_slots[a], phi_slots[b]) for b in range(3)], 1) for a in range(3)]
     )
-    energy_full = lax.dot_general(
-        applied_block, orbital_block, (((1,), (1,)), ((), ())), preferred_element_type=jnp.float32
+    energy_full = jnp.stack(
+        [
+            jnp.stack([pair_product(applied_slots[a], phi_slots[b]) for b in range(3)], 1)
+            for a in range(3)
+        ]
     )
-    gram_full = gram_full.reshape(3, block_orbs, 3, block_orbs)
-    energy_full = energy_full.reshape(3, block_orbs, 3, block_orbs)
-    gram_part, energy_part = (
-        lax.psum_scatter(gram_full, "mat", scatter_dimension=1, tiled=True),
-        lax.psum_scatter(energy_full, "mat", scatter_dimension=1, tiled=True),
-    )
+    gram_part = lax.psum_scatter(gram_full, "mat", scatter_dimension=1, tiled=True)
+    energy_part = lax.psum_scatter(energy_full, "mat", scatter_dimension=1, tiled=True)
     col_count = block_orbs // mat_count
     strips = jnp.stack([gram_part, energy_part])
     assembled = jnp.pad(strips[:, :, :, 1], ((0, 0), (1, 1), (0, 0), (0, 0)))

time: 276 us -> 172 us (0.62)
  waiting for transfers between devices: 126 us -> 65.8 us
  local copies, waits for them, and re-layouts: 41.1 us -> 3.11 us
  other arithmetic: 50 us -> 41.6 us
  starting transfers between devices: 21.5 us -> 25.7 us
    reduce_scatter x1, waiting for transfers between devices: 36.7 us -> 0.02 us  [on_device(): lax.psum_scatter(gram_full, 'mat', scatter_dimension=1, tiled=True)]
    ppermute x4 -> x6, waiting for transfers between devices: 56.3 us -> 25.9 us  [passed_along(): return lax.ppermute(block, axis, route)]
    convert_element_type x0 -> x1, other arithmetic: none -> 21.7 us  [on_device(): applied = stencil(rimmed, potential_window).astype(jnp.bfloat16)]
    another operation x2 -> x7, other arithmetic: 25.1 us -> 3.55 us  [the longest x3 1.8 us: on_device(): jnp.stack([jnp.stack([pair_product(phi_slots[a], phi_slots[b]) for b in r...]
    dot_general x2 -> x0, local copies, waits for them, and re-layouts: 20.6 us -> none  [the longest x1 10.3 us: on_device(): lax.dot_general(orbital_block, orbital_block, (((1,), (1,)), ((), ())), p...]
    slice x3 -> x2, local copies, waits for them, and re-layouts: 20.3 us -> 2.98 us  [the longest x1 2.5 us: on_device(): applied[:, upper_start:]]
    reduce_scatter x1, waiting for transfers between devices: 21.7 us -> 33.2 us  [on_device(): lax.psum_scatter(energy_full, 'mat', scatter_dimension=1, tiled=True)]
    concatenate x1 -> x0, other arithmetic: 9.87 us -> none  [on_device(): slot_stack = jnp.concatenate([received[0], middle, received[1]], axis=1)]
  transfers between devices with their start and end apart: 10 -> 12, of which waited for: 9 -> 6; matrix products, arithmetic and copies ran while one was open for 4% -> 33% of each run, Pallas kernels for 0% -> 0%
where the time goes in v1:
time: 172 us; the launch traced here: 171 us
  waiting for transfers between devices  65.8 us (38%)
  other arithmetic  41.6 us (24%)
  starting transfers between devices  25.7 us (15%)
  matrix products  20.3 us (12%)
  between operations  14.4 us (8%)
  local copies, waits for them, and re-layouts  3.11 us (2%)
    reduce_scatter x1, waiting for transfers between devices, on_device(): lax.psum_scatter(energy_full, 'mat', scatter_dimension=1, tiled=True)  33.2 us
    ppermute x6, waiting for transfers between devices, passed_along(): return lax.ppermute(block, axis, route)  25.9 us
    convert_element_type x1, other arithmetic, on_device(): applied = stencil(rimmed, potential_window).astype(jnp.bfloat16)  21.7 us
    dot_general x18, matrix products, pair_product(): lax.dot_general(left, right, (((1, 2, 3), (1, 2, 3)), ((), ())), preferre...  19 us
    ppermute x6, starting transfers between devices, passed_along(): return lax.ppermute(block, axis, route)  15.6 us
    ppermute x2, starting transfers between devices, extended_2(): after = lax.ppermute(first, axis, down)  9.37 us
    convert_element_type x1, other arithmetic, stencil(): centre_cells = extended[:, 1:-1, 1:-1, :].astype(jnp.float32)  8.07 us
    ppermute x2, waiting for transfers between devices, extended_2(): before = lax.ppermute(last, axis, up)  4.95 us
  transfers between devices with their start and end apart: 12, of which 6 were waited for; matrix products, arithmetic and copies ran while one was open for 33% of the time, Pallas kernels for 0%

profile of v1, /device:TPU:6, one launch (start us, length us, event | category | flops | bytes accessed | tf_op | source)
XLA Modules:
  0.0 171.0 jit_solution(2102566713420577177)
XLA Ops:
  7.3 7.8 %collective-permute-start.5 = (f32[4,8,128]{2,1,0:T(8,128)}, f32[4,8,128]{2,1,0:T(8,128)S(1)}, u32[]{:S(2)}, u32[]{:S(2)}) collective-permute-start(f32[4,8,128]{2,1,0:T(8,128)} %param.7), channel_id=1, source_target_pairs={{4,0},{8,4},{12,8},{16,12},{20,16},{24,20},{28,24},{32,28},{36,32}... | collective-permute-start | bytes 49160 | tf_op jit(solution)/shard_map/ppermute | solution.py:15
  15.8 0.8 subtract_multiply_fusion
  16.6 0.8 fusion.31
  17.4 8.1 %fusion.39 = (f32[256,12,8,128]{3,0,2,1:T(8,128)}, bf16[256,12,8,128]{3,0,2,1:T(8,128)(2,1)S(1)}) fusion(bf16[256,12,8,128]{3,2,1,0:T(8,128)(2,1)} %param.6, pred[12]{0:T(512)(128)(4,1)S(1)} %compare_and_fusion, s32[256,128]{1,0:T(8,128)S(1)} %subtract_multiply_fusion, s32[256,12,8]{0,2,1:T(8,128)S(1)} %broadcast_add_fusion), kind=kLoop, calls=%fused_computation.102 | loop fusion | flops 15728640 | bytes 25395212 | tf_op jit(solution)/shard_map/convert_element_type | solution.py:54
  26.1 1.5 collective-permute-start.3
  29.0 5.3 %collective-permute-start.1 = (bf16[256,4,8,128]{3,0,2,1:T(8,128)(2,1)S(1)}, bf16[256,4,8,128]{3,0,2,1:T(8,128)(2,1)S(1)}, u32[]{:S(2)}, u32[]{:S(2)}) collective-permute-start(bf16[256,4,8,128]{3,0,2,1:T(8,128)(2,1)S(1)} %get-tuple-element.7), channel_id=1, source_target_pairs={{4,0},{8,4},{12,8},{16,12},{20,16},{24,20},{28,24},{32,28},{36,32}... | collective-permute-start | bytes 6291464 | tf_op jit(solution)/shard_map/ppermute | solution.py:23
  34.3 4.9 %collective-permute-done.2 = bf16[256,12,1,128]{3,0,2,1:T(8,128)(2,1)S(1)} collective-permute-done((bf16[256,12,1,128]{3,0,2,1:T(8,128)(2,1)S(1)}, bf16[256,12,1,128]{3,0,2,1:T(8,128)(2,1)S(1)}, u32[]{:S(2)}, u32[]{:S(2)}) %collective-permute-start.2) | collective-permute-done | bytes 786464 | tf_op jit(solution)/shard_map/ppermute | solution.py:14
  39.3 1.7 collective-permute-done.3
  41.0 4.5 %fusion.13 = bf16[256,14,10,128]{3,0,2,1:T(8,128)(2,1)} fusion(bf16[256,12,1,128]{3,0,2,1:T(8,128)(2,1)S(1)} %collective-permute-done.3, bf16[256,12,8,128]{3,0,2,1:T(8,128)(2,1)S(1)} %get-tuple-element.3, bf16[256,12,1,128]{3,0,2,1:T(8,128)(2,1)S(1)} %collective-permute-done.2), kind=kLoop, calls=%fused_computation.18 | loop fusion | flops 55050240 | bytes 17039360 | tf_op jit(solution)/shard_map/concatenate | solution.py:16
  45.5 21.7 %fusion.6 = bf16[256,12,8,128]{3,0,2,1:T(8,128)(2,1)} fusion(f32[256,12,8,128]{3,0,2,1:T(8,128)} %get-tuple-element.2, bf16[256,12,8,128]{3,0,2,1:T(8,128)(2,1)S(1)} %get-tuple-element.3, bf16[256,12,1,128]{3,0,2,1:T(8,128)(2,1)S(1)} %collective-permute-done.2, bf16[256,12,1,128]{3,0,2,1:T(8,128)(2,1)S(1)} %collective-permute-done.3, ...), kind=kLoop, calls=%fused_computation.10 | loop fusion | flops 53477376 | bytes 39370752 | tf_op jit(solution)/shard_map/convert_element_type | solution.py:102
  73.4 1.6 pad_maximum_fusion.2
  75.1 2.5 %fusion.41 = (bf16[256,4,8,128]{3,0,2,1:T(8,128)(2,1)S(1)}, bf16[256,4,8,128]{3,0,2,1:T(8,128)(2,1)S(1)}) fusion(bf16[256,12,8,128]{3,0,2,1:T(8,128)(2,1)} %fusion.6), kind=kLoop, calls=%fused_computation.103 | loop fusion | bytes 8388608 | tf_op jit(solution)/shard_map/slice | solution.py:104
  77.7 5.1 %collective-permute-start.7 = (bf16[256,4,8,128]{3,0,2,1:T(8,128)(2,1)S(1)}, bf16[256,4,8,128]{3,0,2,1:T(8,128)(2,1)S(1)}, u32[]{:S(2)}, u32[]{:S(2)}) collective-permute-start(bf16[256,4,8,128]{3,0,2,1:T(8,128)(2,1)S(1)} %get-tuple-element.5), channel_id=1, source_target_pairs={{4,0},{8,4},{12,8},{16,12},{20,16},{24,20},{28,24},{32,28},{36,32}... | collective-permute-start | bytes 6291464 | tf_op jit(solution)/shard_map/ppermute | solution.py:23
  82.8 3.0 %convolution_bitcast_fusion.2 = f32[256,1,256]{2,0,1:T(8,128)S(1)} fusion(bf16[256,12,8,128]{3,0,2,1:T(8,128)(2,1)} %fusion.6, bf16[256,12,8,128]{3,0,2,1:T(8,128)(2,1)} %copy-done.2), kind=kOutput, calls=%fused_computation.29 | convolution fusion | flops 536870912 | bytes 8650752 | tf_op jit(solution)/shard_map/dot_general | solution.py:69
  85.7 2.5 %convolution_bitcast_fusion.3 = f32[256,1,256]{2,0,1:T(8,128)S(1)} fusion(bf16[256,12,8,128]{3,0,2,1:T(8,128)(2,1)} %fusion.6, bf16[256,4,8,128]{3,0,2,1:T(8,128)(2,1)S(1)} %collective-permute-done), kind=kOutput, calls=%fused_computation.30 | convolution fusion | flops 536870912 | bytes 8650752 | tf_op jit(solution)/shard_map/dot_general | solution.py:69
  88.2 2.5 %convolution_bitcast_fusion.1 = f32[256,1,256]{2,0,1:T(8,128)S(1)} fusion(bf16[256,12,8,128]{3,0,2,1:T(8,128)(2,1)} %fusion.6, bf16[256,4,8,128]{3,0,2,1:T(8,128)(2,1)S(1)} %copy-done.1), kind=kOutput, calls=%fused_computation.28 | convolution fusion | flops 536870912 | bytes 8650752 | tf_op jit(solution)/shard_map/dot_general | solution.py:69
  90.8 15.6 %collective-permute-done.6 = bf16[256,4,8,128]{3,0,2,1:T(8,128)(2,1)S(1)} collective-permute-done((bf16[256,4,8,128]{3,0,2,1:T(8,128)(2,1)S(1)}, bf16[256,4,8,128]{3,0,2,1:T(8,128)(2,1)S(1)}, u32[]{:S(2)}, u32[]{:S(2)}) %collective-permute-start.6) | collective-permute-done | bytes 2097184 | tf_op jit(solution)/shard_map/ppermute | solution.py:23
  111.1 1.6 pad_maximum_fusion.3
  112.8 33.2 %reduce-scatter.5.cloned.1.call-done = f32[3,64,3,256]{3,1,2,0:T(8,128)} async-done(((f32[3,256,3,256]{3,1,2,0:T(8,128)}), f32[3,64,3,256]{3,1,2,0:T(8,128)}) %reduce-scatter.5.cloned.1.call-update) | async-done | bytes 589840 | tf_op jit(solution)/shard_map/reduce_scatter | solution.py:118
  145.9 1.4 fusion.23
  147.4 5.0 %collective-permute-start.8 = (f32[2,3,64,256]{3,2,1,0:T(8,128)S(1)}, f32[2,3,64,256]{3,2,1,0:T(8,128)S(1)}, u32[]{:S(2)}, u32[]{:S(2)}) collective-permute-start(f32[2,3,64,256]{3,2,1,0:T(8,128)S(1)} %get-tuple-element.12), channel_id=1, source_target_pairs={{4,0},{8,4},{12,8},{16,12},{20,16},{24,20},{28,24},{32,28},{36,32}... | collective-permute-start | bytes 1179656 | tf_op jit(solution)/shard_map/ppermute | solution.py:23
  152.7 5.1 %collective-permute-done.8 = f32[2,3,64,256]{3,2,1,0:T(8,128)S(1)} collective-permute-done((f32[2,3,64,256]{3,2,1,0:T(8,128)S(1)}, f32[2,3,64,256]{3,2,1,0:T(8,128)S(1)}, u32[]{:S(2)}, u32[]{:S(2)}) %collective-permute-start.8) | collective-permute-done | bytes 393248 | tf_op jit(solution)/shard_map/ppermute | solution.py:23
  157.7 5.2 %collective-permute-done.9 = f32[2,3,64,256]{3,2,1,0:T(8,128)S(1)} collective-permute-done((f32[2,3,64,256]{3,2,1,0:T(8,128)S(1)}, f32[2,3,64,256]{3,2,1,0:T(8,128)S(1)}, u32[]{:S(2)}, u32[]{:S(2)}) %collective-permute-start.9) | collective-permute-done | bytes 393248 | tf_op jit(solution)/shard_map/ppermute | solution.py:23
  163.0 1.1 fusion.25
  (62 shorter events, 14.0 us)
Async XLA Ops:
  7.2 105.6 %reduce-scatter.3.cloned.1.call-start = ((), (), s32[]{:S(2)}) async-start(), calls=%async_computation.2 | async-start | bytes 2949120 | tf_op jit(solution)/shard_map/reduce_scatter | solution.py:117
  7.2 21.8 %collective-permute-start.4 = (f32[4,8,128]{2,1,0:T(8,128)}, f32[4,8,128]{2,1,0:T(8,128)S(1)}, u32[]{:S(2)}, u32[]{:S(2)}) collective-permute-start(f32[4,8,128]{2,1,0:T(8,128)} %param.7), channel_id=1, source_target_pairs={{0,4},{4,8},{8,12},{12,16},{16,20},{20,24},{24,28},{28,32},{32,36}... | collective-permute-start | bytes 49160 | tf_op jit(solution)/shard_map/ppermute | solution.py:14
  7.3 27.0 %collective-permute-start.5 = (f32[4,8,128]{2,1,0:T(8,128)}, f32[4,8,128]{2,1,0:T(8,128)S(1)}, u32[]{:S(2)}, u32[]{:S(2)}) collective-permute-start(f32[4,8,128]{2,1,0:T(8,128)} %param.7), channel_id=1, source_target_pairs={{4,0},{8,4},{12,8},{16,12},{20,16},{24,20},{28,24},{32,28},{36,32}... | collective-permute-start | bytes 49160 | tf_op jit(solution)/shard_map/ppermute | solution.py:15
  25.5 46.3 %copy-start.2 = (bf16[256,12,8,128]{3,0,2,1:T(8,128)(2,1)}, bf16[256,12,8,128]{3,0,2,1:T(8,128)(2,1)S(1)}, u32[]{:S(2)}) copy-start(bf16[256,12,8,128]{3,0,2,1:T(8,128)(2,1)S(1)} %get-tuple-element.3) | copy-start | bytes 18874372
  25.6 13.7 %collective-permute-start.2 = (bf16[256,12,1,128]{3,0,2,1:T(8,128)(2,1)S(1)}, bf16[256,12,1,128]{3,0,2,1:T(8,128)(2,1)S(1)}, u32[]{:S(2)}, u32[]{:S(2)}) collective-permute-start(bf16[256,12,1,128]{3,0,2,1:T(8,128)(2,1)S(1)} %get-tuple-element.9), channel_id=1, source_target_pairs={{0,1},{1,2},{2,3},{3,0},{4,5},{5,6},{6,7},{7,4},{8,9},{9,10},{10,1... | collective-permute-start | bytes 2359304 | tf_op jit(solution)/shard_map/ppermute | solution.py:14
  26.1 14.9 %collective-permute-start.3 = (bf16[256,12,1,128]{3,0,2,1:T(8,128)(2,1)S(1)}, bf16[256,12,1,128]{3,0,2,1:T(8,128)(2,1)S(1)}, u32[]{:S(2)}, u32[]{:S(2)}) collective-permute-start(bf16[256,12,1,128]{3,0,2,1:T(8,128)(2,1)S(1)} %get-tuple-element.8), channel_id=1, source_target_pairs={{1,0},{2,1},{3,2},{0,3},{5,4},{6,5},{7,6},{4,7},{9,8},{10,9},{11,1... | collective-permute-start | bytes 2359304 | tf_op jit(solution)/shard_map/ppermute | solution.py:15
  28.2 6.2 %copy-start.3 = (f32[4,8,128]{2,1,0:T(8,128)S(1)}, f32[4,8,128]{2,1,0:T(8,128)}, u32[]{:S(2)}) copy-start(f32[4,8,128]{2,1,0:T(8,128)} %param.7) | copy-start | bytes 49156
  28.2 40.5 %collective-permute-start = (bf16[256,4,8,128]{3,0,2,1:T(8,128)(2,1)S(1)}, bf16[256,4,8,128]{3,0,2,1:T(8,128)(2,1)S(1)}, u32[]{:S(2)}, u32[]{:S(2)}) collective-permute-start(bf16[256,4,8,128]{3,0,2,1:T(8,128)(2,1)S(1)} %get-tuple-element.6), channel_id=1, source_target_pairs={{252,0},{0,4},{4,8},{8,12},{12,16},{16,20},{20,24},{24,28},{28,32}... | collective-permute-start | bytes 6291464 | tf_op jit(solution)/shard_map/ppermute | solution.py:23
  29.0 38.2 %collective-permute-start.1 = (bf16[256,4,8,128]{3,0,2,1:T(8,128)(2,1)S(1)}, bf16[256,4,8,128]{3,0,2,1:T(8,128)(2,1)S(1)}, u32[]{:S(2)}, u32[]{:S(2)}) collective-permute-start(bf16[256,4,8,128]{3,0,2,1:T(8,128)(2,1)S(1)} %get-tuple-element.7), channel_id=1, source_target_pairs={{4,0},{8,4},{12,8},{16,12},{20,16},{24,20},{28,24},{32,28},{36,32}... | collective-permute-start | bytes 6291464 | tf_op jit(solution)/shard_map/ppermute | solution.py:23
  67.2 3.8 %copy-start = (bf16[256,4,8,128]{3,0,2,1:T(8,128)(2,1)}, bf16[256,4,8,128]{3,0,2,1:T(8,128)(2,1)S(1)}, u32[]{:S(2)}) copy-start(bf16[256,4,8,128]{3,0,2,1:T(8,128)(2,1)S(1)} %collective-permute-done.1) | copy-start | bytes 6291460
  75.1 70.9 %reduce-scatter.5.cloned.1.call-start = ((), (), s32[]{:S(2)}) async-start(), calls=%async_computation.3 | async-start | bytes 2949120 | tf_op jit(solution)/shard_map/reduce_scatter | solution.py:118
  77.6 28.9 %collective-permute-start.6 = (bf16[256,4,8,128]{3,0,2,1:T(8,128)(2,1)S(1)}, bf16[256,4,8,128]{3,0,2,1:T(8,128)(2,1)S(1)}, u32[]{:S(2)}, u32[]{:S(2)}) collective-permute-start(bf16[256,4,8,128]{3,0,2,1:T(8,128)(2,1)S(1)} %get-tuple-element.4), channel_id=1, source_target_pairs={{252,0},{0,4},{4,8},{8,12},{12,16},{16,20},{20,24},{24,28},{28,32}... | collective-permute-start | bytes 6291464 | tf_op jit(solution)/shard_map/ppermute | solution.py:23
  77.7 31.1 %collective-permute-start.7 = (bf16[256,4,8,128]{3,0,2,1:T(8,128)(2,1)S(1)}, bf16[256,4,8,128]{3,0,2,1:T(8,128)(2,1)S(1)}, u32[]{:S(2)}, u32[]{:S(2)}) collective-permute-start(bf16[256,4,8,128]{3,0,2,1:T(8,128)(2,1)S(1)} %get-tuple-element.5), channel_id=1, source_target_pairs={{4,0},{8,4},{12,8},{16,12},{20,16},{24,20},{28,24},{32,28},{36,32}... | collective-permute-start | bytes 6291464 | tf_op jit(solution)/shard_map/ppermute | solution.py:23
  85.7 2.5 %copy-start.1 = (bf16[256,4,8,128]{3,0,2,1:T(8,128)(2,1)S(1)}, bf16[256,4,8,128]{3,0,2,1:T(8,128)(2,1)}, u32[]{:S(2)}) copy-start(bf16[256,4,8,128]{3,0,2,1:T(8,128)(2,1)} %copy-done) | copy-start | bytes 6291460
  88.2 19.7 %slice-start = ((s8[6291456]{0:T(1024)(128)(4,1)}), s8[4194304]{0:T(1024)(128)(4,1)S(1)}, s32[]{:S(2)}) async-start(s8[6291456]{0:T(1024)(128)(4,1)} %bitcast.180), calls=%async_computation.4 | async-start | bytes 8388608
  90.8 17.2 %slice-start.1 = ((s8[6291456]{0:T(1024)(128)(4,1)}), s8[2097152]{0:T(1024)(128)(4,1)S(1)}, s32[]{:S(2)}) async-start(s8[6291456]{0:T(1024)(128)(4,1)} %bitcast.180), calls=%async_computation.5 | async-start | bytes 4194304
  112.7 39.7 %copy-start.4 = (s32[2,5,2]{1,2,0:T(2,128)S(1)}, s32[2,5,2]{1,2,0:T(2,128)}, u32[]{:S(2)}) copy-start(s32[2,5,2]{1,2,0:T(2,128)} %param.11) | copy-start | bytes 244
  147.4 10.3 %collective-permute-start.8 = (f32[2,3,64,256]{3,2,1,0:T(8,128)S(1)}, f32[2,3,64,256]{3,2,1,0:T(8,128)S(1)}, u32[]{:S(2)}, u32[]{:S(2)}) collective-permute-start(f32[2,3,64,256]{3,2,1,0:T(8,128)S(1)} %get-tuple-element.12), channel_id=1, source_target_pairs={{4,0},{8,4},{12,8},{16,12},{20,16},{24,20},{28,24},{32,28},{36,32}... | collective-permute-start | bytes 1179656 | tf_op jit(solution)/shard_map/ppermute | solution.py:23
  152.4 10.5 %collective-permute-start.9 = (f32[2,3,64,256]{3,2,1,0:T(8,128)S(1)}, f32[2,3,64,256]{3,2,1,0:T(8,128)S(1)}, u32[]{:S(2)}, u32[]{:S(2)}) collective-permute-start(f32[2,3,64,256]{3,2,1,0:T(8,128)S(1)} %get-tuple-element.11), channel_id=1, source_target_pairs={{252,0},{0,4},{4,8},{8,12},{12,16},{16,20},{20,24},{24,28},{28,32}... | collective-permute-start | bytes 1179656 | tf_op jit(solution)/shard_map/ppermute | solution.py:23
Sparse Core Ops, SparseCore 0:
  75.2 33.9 reduce-scatter.2
  112.9 33.0 reduce-scatter.4

commit v2 on v1

--- a/solution.py
+++ b/solution.py
@@ -91,19 +91,46 @@
     )
     masked = jnp.where(inside, orbitals, jnp.zeros_like(orbitals))
     upper_start = 2 * patch_cells
+    to_right = masked[:, upper_start - 1 : window_cells - 1]
+    to_left = masked[:, 1 : patch_cells + 1]
+    from_left = passed_along(to_right, "dom", 1)
+    from_right = passed_along(to_left, "dom", -1)
+    mat_size = lax.axis_size("mat")
+    up = [(i, (i + 1) % mat_size) for i in range(mat_size)]
+    down = [(j, i) for i, j in up]
+    row_above = lax.ppermute(masked[:, :, second_cells - 1], "mat", up)
+    row_below = lax.ppermute(masked[:, :, 0], "mat", down)
+    rows_right = jnp.stack(
+        [row_above[:, upper_start - 1 : window_cells - 1], row_below[:, upper_start - 1 : window_cells - 1]]
+    )
+    rows_left = jnp.stack([row_above[:, 1 : patch_cells + 1], row_below[:, 1 : patch_cells + 1]])
+    rows_from_left = passed_along(rows_right, "dom", 1)
+    rows_from_right = passed_along(rows_left, "dom", -1)
+
+    def with_rows(planes, rows):
+        return jnp.concatenate([rows[0][:, :, None], planes, rows[1][:, :, None]], axis=2)
+
+    zero_plane = jnp.zeros_like(masked[:, :1])
+    zero_rows = jnp.zeros((2, block_orbs, 1, third_cells), masked.dtype)
+    own_ext = with_rows(
+        masked[:, patch_cells - 1 : upper_start + 1],
+        jnp.stack([row_above[:, patch_cells - 1 : upper_start + 1], row_below[:, patch_cells - 1 : upper_start + 1]]),
+    )
+    left_ext = with_rows(
+        jnp.concatenate([from_left, zero_plane, zero_plane], axis=1),
+        jnp.concatenate([rows_from_left, zero_rows, zero_rows], axis=2),
+    )
+    right_ext = with_rows(
+        jnp.concatenate([zero_plane, zero_plane, from_right], axis=1),
+        jnp.concatenate([zero_rows, zero_rows, rows_from_right], axis=2),
+    )
     phi_slots = [
-        passed_along(masked[:, upper_start:], "dom", 1),
+        jnp.concatenate([from_left[:, 1:], zero_plane], axis=1),
         masked[:, patch_cells:upper_start],
-        passed_along(masked[:, :patch_cells], "dom", -1),
+        jnp.concatenate([zero_plane, from_right[:, :-1]], axis=1),
     ]
-    rimmed = extended_2(masked, (("mat", 2),), 1)
-    rimmed = jnp.pad(rimmed, ((0, 0), (1, 1), (0, 0), (0, 0)))
-    potential_window = extended_2(potential, (("dom", 0),), patch_cells)
-    applied = stencil(rimmed, potential_window).astype(jnp.bfloat16)
     applied_slots = [
-        passed_along(applied[:, upper_start:], "dom", 1),
-        applied[:, patch_cells:upper_start],
-        passed_along(applied[:, :patch_cells], "dom", -1),
+        stencil(ext, potential).astype(jnp.bfloat16) for ext in (left_ext, own_ext, right_ext)
     ]
     gram_full = jnp.stack(
         [jnp.stack([pair_product(phi_slots[a], phi_slots[b]) for b in range(3)], 1) for a in range(3)]

time: 172 us -> 178 us (1.035)
  waiting for transfers between devices: 65.8 us -> 89.7 us
  other arithmetic: 41.6 us -> 25.7 us
  starting transfers between devices: 25.7 us -> 20.2 us
  local copies, waits for them, and re-layouts: 3.11 us -> 7.84 us
    reduce_scatter x1, waiting for transfers between devices: 0.02 us -> 36.7 us  [on_device(): lax.psum_scatter(gram_full, 'mat', scatter_dimension=1, tiled=True)]
    reduce_scatter x1, waiting for transfers between devices: 33.2 us -> 19.2 us  [on_device(): lax.psum_scatter(energy_full, 'mat', scatter_dimension=1, tiled=True)]
    convert_element_type x1 -> x2, other arithmetic: 21.7 us -> 10.3 us  [on_device(): stencil(ext, potential).astype(jnp.bfloat16)]
    ppermute x4 -> x2, starting transfers between devices: 10 us -> 2.37 us  [the longest x1 2.29 us: on_device(): row_above = lax.ppermute(masked[:, :, second_cells - 1], 'mat', up)]
    ppermute x4 -> x2, waiting for transfers between devices: 6.66 us -> 13.8 us  [the longest x1 8.68 us: on_device(): row_above = lax.ppermute(masked[:, :, second_cells - 1], 'mat', up)]
    ppermute x6, waiting for transfers between devices: 25.9 us -> 19.9 us  [passed_along(): return lax.ppermute(block, axis, route)]
    convert_element_type x1 -> x3, other arithmetic: 8.07 us -> 2.05 us  [stencil(): centre_cells = extended[:, 1:-1, 1:-1, :].astype(jnp.float32)]
    select_n x0 -> x1, other arithmetic: none -> 5.94 us  [on_device(): masked = jnp.where(inside, orbitals, jnp.zeros_like(orbitals))]
  transfers between devices with their start and end apart: 12 -> 10, of which waited for: 6 -> 8; matrix products, arithmetic and copies ran while one was open for 33% -> 16% of each run, Pallas kernels for 0% -> 0%
where the time goes in v2:
time: 178 us; the launch traced here: 177 us
  waiting for transfers between devices  89.7 us (50%)
  other arithmetic  25.7 us (14%)
  starting transfers between devices  20.2 us (11%)
  matrix products  18.7 us (11%)
  between operations  14.5 us (8%)
  local copies, waits for them, and re-layouts  7.84 us (4%)
    reduce_scatter x1, waiting for transfers between devices, on_device(): lax.psum_scatter(gram_full, 'mat', scatter_dimension=1, tiled=True)  36.7 us
    ppermute x6, waiting for transfers between devices, passed_along(): return lax.ppermute(block, axis, route)  19.9 us
    reduce_scatter x1, waiting for transfers between devices, on_device(): lax.psum_scatter(energy_full, 'mat', scatter_dimension=1, tiled=True)  19.2 us
    ppermute x6, starting transfers between devices, passed_along(): return lax.ppermute(block, axis, route)  17.5 us
    dot_general x18, matrix products, pair_product(): lax.dot_general(left, right, (((1, 2, 3), (1, 2, 3)), ((), ())), preferre...  17.4 us
    convert_element_type x2, other arithmetic, on_device(): stencil(ext, potential).astype(jnp.bfloat16)  10.3 us
    ppermute x1, waiting for transfers between devices, on_device(): row_above = lax.ppermute(masked[:, :, second_cells - 1], 'mat', up)  8.68 us
    select_n x1, other arithmetic, on_device(): masked = jnp.where(inside, orbitals, jnp.zeros_like(orbitals))  5.94 us
  transfers between devices with their start and end apart: 10, of which 8 were waited for; matrix products, arithmetic and copies ran while one was open for 16% of the time, Pallas kernels for 0%

profile of v2, /device:TPU:6, one launch (start us, length us, event | category | flops | bytes accessed | tf_op | source)
XLA Modules:
  0.0 176.6 jit_solution(7429585750915960057)
XLA Ops:
  9.5 5.9 %fusion.1 = bf16[256,12,8,128]{3,0,2,1:T(8,128)(2,1)S(1)} fusion(bf16[256,12,8,128]{3,2,1,0:T(8,128)(2,1)} %param.6, s32[256,128]{1,0:T(8,128)S(1)} %subtract_multiply_fusion, s32[256,12,8]{0,2,1:T(8,128)S(1)} %broadcast_add_fusion, pred[12]{0:T(512)(128)(4,1)S(1)} %compare_and_fusion), kind=kLoop, calls=%fused_computation.2 | loop fusion | flops 12582912 | bytes 12812300 | tf_op jit(solution)/shard_map/jit(_where)/select_n | solution.py:92
  15.6 2.3 %collective-permute-start.2 = (bf16[256,12,128]{2,0,1:T(8,128)(2,1)S(1)}, bf16[256,12,128]{2,0,1:T(8,128)(2,1)S(1)}, u32[]{:S(2)}, u32[]{:S(2)}) collective-permute-start(bf16[256,12,128]{2,0,1:T(8,128)(2,1)S(1)} %get-tuple-element.5), channel_id=1, source_target_pairs={{0,1},{1,2},{2,3},{3,0},{4,5},{5,6},{6,7},{7,4},{8,9},{9,10},{10,1... | collective-permute-start | bytes 2359304 | tf_op jit(solution)/shard_map/ppermute | solution.py:101
  17.9 1.2 slice_convert_fusion.2
  19.3 7.0 %collective-permute-start.1 = (bf16[256,4,8,128]{3,0,2,1:T(8,128)(2,1)S(1)}, bf16[256,4,8,128]{3,0,2,1:T(8,128)(2,1)S(1)}, u32[]{:S(2)}, u32[]{:S(2)}) collective-permute-start(bf16[256,4,8,128]{3,0,2,1:T(8,128)(2,1)S(1)} %get-tuple-element.3), channel_id=1, source_target_pairs={{4,0},{8,4},{12,8},{16,12},{20,16},{24,20},{28,24},{32,28},{36,32}... | collective-permute-start | bytes 6291464 | tf_op jit(solution)/shard_map/ppermute | solution.py:23
  26.3 8.7 %collective-permute-done.2 = bf16[256,12,128]{2,0,1:T(8,128)(2,1)S(1)} collective-permute-done((bf16[256,12,128]{2,0,1:T(8,128)(2,1)S(1)}, bf16[256,12,128]{2,0,1:T(8,128)(2,1)S(1)}, u32[]{:S(2)}, u32[]{:S(2)}) %collective-permute-start.2) | collective-permute-done | bytes 786464 | tf_op jit(solution)/shard_map/ppermute | solution.py:101
  35.0 5.1 %collective-permute-done.3 = bf16[256,12,128]{2,0,1:T(8,128)(2,1)S(1)} collective-permute-done((bf16[256,12,128]{2,0,1:T(8,128)(2,1)S(1)}, bf16[256,12,128]{2,0,1:T(8,128)(2,1)S(1)}, u32[]{:S(2)}, u32[]{:S(2)}) %collective-permute-start.3) | collective-permute-done | bytes 786464 | tf_op jit(solution)/shard_map/ppermute | solution.py:102
  40.4 5.3 %collective-permute-start.5 = (bf16[2,256,4,128]{3,1,2,0:T(8,128)(2,1)S(1)}, bf16[2,256,4,128]{3,1,2,0:T(8,128)(2,1)S(1)}, u32[]{:S(2)}, u32[]{:S(2)}) collective-permute-start(bf16[2,256,4,128]{3,1,2,0:T(8,128)(2,1)S(1)} %pad_maximum_fusion.9), channel_id=1, source_target_pairs={{4,0},{8,4},{12,8},{16,12},{20,16},{24,20},{28,24},{32,28},{36,32}... | collective-permute-start | bytes 1572872 | tf_op jit(solution)/shard_map/ppermute | solution.py:23
  45.8 8.5 %collective-permute-done.4 = bf16[2,256,4,128]{3,1,2,0:T(8,128)(2,1)S(1)} collective-permute-done((bf16[2,256,4,128]{3,1,2,0:T(8,128)(2,1)S(1)}, bf16[2,256,4,128]{3,1,2,0:T(8,128)(2,1)S(1)}, u32[]{:S(2)}, u32[]{:S(2)}) %collective-permute-start.4) | collective-permute-done | bytes 524320 | tf_op jit(solution)/shard_map/ppermute | solution.py:23
  54.3 1.1 collective-permute-done.5
  56.7 1.3 slice.175
  59.2 1.0 slice-done.4
  60.2 7.0 %fusion.7 = (bf16[256,4,8,128]{3,0,2,1:T(8,128)(2,1)S(1)}, bf16[256,4,8,128]{3,0,2,1:T(8,128)(2,1)}) fusion(f32[256,4,8,128]{3,0,2,1:T(8,128)S(1)} %slice_convert_fusion.1, bf16[256,4,8,128]{3,0,2,1:T(8,128)(2,1)S(1)} %collective-permute-done, bf16[256,6,8,128]{3,0,2,1:T(8,128)(2,1)S(1)} %concatenate.41, bf16[256,6,1,128]{3,0,2,1:T(8,128)(2,1)S(1)} %get-tuple-element.17, ...), kind=kLoop, calls=%fused_computation.14 | loop fusion | flops 35651584 | bytes 28852224 | tf_op jit(solution)/shard_map/convert_element_type | solution.py:133
  67.2 2.9 %fusion.50 = f32[256,1,256]{2,0,1:T(8,128)S(1)} fusion(bf16[256,4,8,128]{3,0,2,1:T(8,128)(2,1)} %get-tuple-element.21, bf16[256,3,8,128]{3,0,2,1:T(8,128)(2,1)} %slice.175), kind=kOutput, calls=%fused_computation.69 | convolution fusion | flops 536870912 | bytes 3932160 | tf_op jit(solution)/shard_map/dot_general | solution.py:69
  76.1 3.3 %fusion.19 = bf16[256,4,8,128]{3,0,2,1:T(8,128)(2,1)S(1)} fusion(f32[256,4,8,128]{3,0,2,1:T(8,128)S(1)} %slice_convert_fusion, bf16[256,4,8,128]{3,0,2,1:T(8,128)(2,1)S(1)} %collective-permute-done.1, bf16[256,6,8,128]{3,0,2,1:T(8,128)(2,1)S(1)} %concatenate.47, bf16[256,6,1,128]{3,0,2,1:T(8,128)(2,1)S(1)} %copy-done.7, ...), kind=kLoop, calls=%fused_computation.26 | loop fusion | flops 17825792 | bytes 14434304 | tf_op jit(solution)/shard_map/convert_element_type | solution.py:133
  81.8 1.6 pad_maximum_fusion.1
  83.7 3.1 %convolution_bitcast_fusion.1 = f32[256,1,256]{2,0,1:T(8,128)S(1)} fusion(bf16[256,12,8,128]{3,0,2,1:T(8,128)(2,1)} %copy-done), kind=kOutput, calls=%fused_computation.66 | convolution fusion | flops 536870912 | bytes 8650752 | tf_op jit(solution)/shard_map/dot_general | solution.py:69
  94.0 1.6 pad_maximum_fusion
  95.7 19.2 %reduce-scatter.5.cloned.1.call-done = f32[3,64,3,256]{3,1,2,0:T(8,128)} async-done(((f32[3,256,3,256]{3,1,2,0:T(8,128)}), f32[3,64,3,256]{3,1,2,0:T(8,128)}) %reduce-scatter.5.cloned.1.call-update) | async-done | bytes 589840 | tf_op jit(solution)/shard_map/reduce_scatter | solution.py:145
  114.9 36.7 %reduce-scatter.3.cloned.1.call-done = f32[3,64,3,256]{3,1,2,0:T(8,128)} async-done(((f32[3,256,3,256]{3,1,2,0:T(8,128)}), f32[3,64,3,256]{3,1,2,0:T(8,128)}) %reduce-scatter.3.cloned.1.call-update) | async-done | bytes 589840 | tf_op jit(solution)/shard_map/reduce_scatter | solution.py:144
  151.6 1.4 fusion.93
  153.1 5.0 %collective-permute-start.6 = (f32[2,3,64,256]{3,2,1,0:T(8,128)S(1)}, f32[2,3,64,256]{3,2,1,0:T(8,128)S(1)}, u32[]{:S(2)}, u32[]{:S(2)}) collective-permute-start(f32[2,3,64,256]{3,2,1,0:T(8,128)S(1)} %get-tuple-element.9), channel_id=1, source_target_pairs={{4,0},{8,4},{12,8},{16,12},{20,16},{24,20},{28,24},{32,28},{36,32}... | collective-permute-start | bytes 1179656 | tf_op jit(solution)/shard_map/ppermute | solution.py:23
  158.3 5.1 %collective-permute-done.6 = f32[2,3,64,256]{3,2,1,0:T(8,128)S(1)} collective-permute-done((f32[2,3,64,256]{3,2,1,0:T(8,128)S(1)}, f32[2,3,64,256]{3,2,1,0:T(8,128)S(1)}, u32[]{:S(2)}, u32[]{:S(2)}) %collective-permute-start.6) | collective-permute-done | bytes 393248 | tf_op jit(solution)/shard_map/ppermute | solution.py:23
  163.4 5.2 %collective-permute-done.7 = f32[2,3,64,256]{3,2,1,0:T(8,128)S(1)} collective-permute-done((f32[2,3,64,256]{3,2,1,0:T(8,128)S(1)}, f32[2,3,64,256]{3,2,1,0:T(8,128)S(1)}, u32[]{:S(2)}, u32[]{:S(2)}) %collective-permute-start.7) | collective-permute-done | bytes 393248 | tf_op jit(solution)/shard_map/ppermute | solution.py:23
  168.7 1.1 fusion.95
  (86 shorter events, 21.4 us)
Async XLA Ops:
  7.2 107.7 %reduce-scatter.5.cloned.1.call-start = ((), (), s32[]{:S(2)}) async-start(), calls=%async_computation.3 | async-start | bytes 2949120 | tf_op jit(solution)/shard_map/reduce_scatter | solution.py:145
  15.4 10.8 %copy-start = (bf16[256,12,8,128]{3,0,2,1:T(8,128)(2,1)}, bf16[256,12,8,128]{3,0,2,1:T(8,128)(2,1)S(1)}, u32[]{:S(2)}) copy-start(bf16[256,12,8,128]{3,0,2,1:T(8,128)(2,1)S(1)} %fusion.1) | copy-start | bytes 18874372
  15.6 19.4 %collective-permute-start.2 = (bf16[256,12,128]{2,0,1:T(8,128)(2,1)S(1)}, bf16[256,12,128]{2,0,1:T(8,128)(2,1)S(1)}, u32[]{:S(2)}, u32[]{:S(2)}) collective-permute-start(bf16[256,12,128]{2,0,1:T(8,128)(2,1)S(1)} %get-tuple-element.5), channel_id=1, source_target_pairs={{0,1},{1,2},{2,3},{3,0},{4,5},{5,6},{6,7},{7,4},{8,9},{9,10},{10,1... | collective-permute-start | bytes 2359304 | tf_op jit(solution)/shard_map/ppermute | solution.py:101
  19.1 37.2 %collective-permute-start = (bf16[256,4,8,128]{3,0,2,1:T(8,128)(2,1)S(1)}, bf16[256,4,8,128]{3,0,2,1:T(8,128)(2,1)S(1)}, u32[]{:S(2)}, u32[]{:S(2)}) collective-permute-start(bf16[256,4,8,128]{3,0,2,1:T(8,128)(2,1)S(1)} %get-tuple-element.4), channel_id=1, source_target_pairs={{252,0},{0,4},{4,8},{8,12},{12,16},{16,20},{20,24},{24,28},{28,32}... | collective-permute-start | bytes 6291464 | tf_op jit(solution)/shard_map/ppermute | solution.py:23
  19.2 20.9 %collective-permute-start.3 = (bf16[256,12,128]{2,0,1:T(8,128)(2,1)S(1)}, bf16[256,12,128]{2,0,1:T(8,128)(2,1)S(1)}, u32[]{:S(2)}, u32[]{:S(2)}) collective-permute-start(bf16[256,12,128]{2,0,1:T(8,128)(2,1)S(1)} %get-tuple-element.6), channel_id=1, source_target_pairs={{1,0},{2,1},{3,2},{0,3},{5,4},{6,5},{7,6},{4,7},{9,8},{10,9},{11,1... | collective-permute-start | bytes 2359304 | tf_op jit(solution)/shard_map/ppermute | solution.py:102
  19.3 53.9 %collective-permute-start.1 = (bf16[256,4,8,128]{3,0,2,1:T(8,128)(2,1)S(1)}, bf16[256,4,8,128]{3,0,2,1:T(8,128)(2,1)S(1)}, u32[]{:S(2)}, u32[]{:S(2)}) collective-permute-start(bf16[256,4,8,128]{3,0,2,1:T(8,128)(2,1)S(1)} %get-tuple-element.3), channel_id=1, source_target_pairs={{4,0},{8,4},{12,8},{16,12},{20,16},{24,20},{28,24},{32,28},{36,32}... | collective-permute-start | bytes 6291464 | tf_op jit(solution)/shard_map/ppermute | solution.py:23
  40.2 14.0 %collective-permute-start.4 = (bf16[2,256,4,128]{3,1,2,0:T(8,128)(2,1)S(1)}, bf16[2,256,4,128]{3,1,2,0:T(8,128)(2,1)S(1)}, u32[]{:S(2)}, u32[]{:S(2)}) collective-permute-start(bf16[2,256,4,128]{3,1,2,0:T(8,128)(2,1)S(1)} %pad_maximum_fusion.8), channel_id=1, source_target_pairs={{252,0},{0,4},{4,8},{8,12},{12,16},{16,20},{20,24},{24,28},{28,32}... | collective-permute-start | bytes 1572872 | tf_op jit(solution)/shard_map/ppermute | solution.py:23
  40.4 15.1 %collective-permute-start.5 = (bf16[2,256,4,128]{3,1,2,0:T(8,128)(2,1)S(1)}, bf16[2,256,4,128]{3,1,2,0:T(8,128)(2,1)S(1)}, u32[]{:S(2)}, u32[]{:S(2)}) collective-permute-start(bf16[2,256,4,128]{3,1,2,0:T(8,128)(2,1)S(1)} %pad_maximum_fusion.9), channel_id=1, source_target_pairs={{4,0},{8,4},{12,8},{16,12},{20,16},{24,20},{28,24},{32,28},{36,32}... | collective-permute-start | bytes 1572872 | tf_op jit(solution)/shard_map/ppermute | solution.py:23
  54.3 4.3 %slice-start = ((s8[6291456]{0:T(1024)(128)(4,1)}), s8[4194304]{0:T(1024)(128)(4,1)S(1)}, s32[]{:S(2)}) async-start(s8[6291456]{0:T(1024)(128)(4,1)} %bitcast.202), calls=%async_computation.4 | async-start | bytes 8388608
  56.3 3.0 %slice-start.1 = ((s8[6291456]{0:T(1024)(128)(4,1)}), s8[2097152]{0:T(1024)(128)(4,1)S(1)}, s32[]{:S(2)}) async-start(s8[6291456]{0:T(1024)(128)(4,1)} %bitcast.202), calls=%async_computation.5 | async-start | bytes 4194304
  56.3 2.3 %copy-start.1 = (bf16[256,4,8,128]{3,0,2,1:T(8,128)(2,1)}, bf16[256,4,8,128]{3,0,2,1:T(8,128)(2,1)S(1)}, u32[]{:S(2)}) copy-start(bf16[256,4,8,128]{3,0,2,1:T(8,128)(2,1)S(1)} %collective-permute-done) | copy-start | bytes 6291460
  58.0 2.1 %slice-start.4 = ((bf16[256,12,8,128]{3,0,2,1:T(8,128)(2,1)}), bf16[256,6,8,128]{3,0,2,1:T(8,128)(2,1)S(1)}, s32[]{:S(2)}) async-start(bf16[256,12,8,128]{3,0,2,1:T(8,128)(2,1)} %copy-done), calls=%async_computation.8 | async-start | bytes 6291456 | tf_op jit(solution)/shard_map/slice | solution.py:116
  58.0 2.1 %copy-start.8 = (f32[4,8,128]{2,1,0:T(8,128)S(1)}, f32[4,8,128]{2,1,0:T(8,128)}, u32[]{:S(2)}) copy-start(f32[4,8,128]{2,1,0:T(8,128)} %param.7) | copy-start | bytes 49156
  67.2 2.9 %copy-start.6 = (bf16[256,3,8,128]{3,0,2,1:T(8,128)(2,1)S(1)}, bf16[256,3,8,128]{3,0,2,1:T(8,128)(2,1)}, u32[]{:S(2)}) copy-start(bf16[256,3,8,128]{3,0,2,1:T(8,128)(2,1)} %slice.175) | copy-start | bytes 4718596
  70.1 1.6 copy-start.5
  73.2 2.5 %copy-start.3 = (bf16[256,4,8,128]{3,0,2,1:T(8,128)(2,1)}, bf16[256,4,8,128]{3,0,2,1:T(8,128)(2,1)S(1)}, u32[]{:S(2)}) copy-start(bf16[256,4,8,128]{3,0,2,1:T(8,128)(2,1)S(1)} %collective-permute-done.1) | copy-start | bytes 6291460
  83.4 68.2 %reduce-scatter.3.cloned.1.call-start = ((), (), s32[]{:S(2)}) async-start(), calls=%async_computation.2 | async-start | bytes 2949120 | tf_op jit(solution)/shard_map/reduce_scatter | solution.py:144
  83.7 3.8 %copy-start.4 = (bf16[256,4,8,128]{3,0,2,1:T(8,128)(2,1)S(1)}, bf16[256,4,8,128]{3,0,2,1:T(8,128)(2,1)}, u32[]{:S(2)}) copy-start(bf16[256,4,8,128]{3,0,2,1:T(8,128)(2,1)} %copy-done.3) | copy-start | bytes 6291460
  83.7 4.6 %slice-start.2 = ((s8[6291456]{0:T(1024)(128)(4,1)}), s8[4194304]{0:T(1024)(128)(4,1)S(1)}, s32[]{:S(2)}) async-start(s8[6291456]{0:T(1024)(128)(4,1)} %bitcast.204), calls=%async_computation.6 | async-start | bytes 8388608
  86.8 1.8 %slice-start.3 = ((s8[6291456]{0:T(1024)(128)(4,1)}), s8[2097152]{0:T(1024)(128)(4,1)S(1)}, s32[]{:S(2)}) async-start(s8[6291456]{0:T(1024)(128)(4,1)} %bitcast.204), calls=%async_computation.7 | async-start | bytes 4194304
  89.4 1.6 copy-start.2
  95.6 62.5 %copy-start.9 = (s32[2,5,2]{1,2,0:T(2,128)S(1)}, s32[2,5,2]{1,2,0:T(2,128)}, u32[]{:S(2)}) copy-start(s32[2,5,2]{1,2,0:T(2,128)} %param.11) | copy-start | bytes 244
  153.1 10.3 %collective-permute-start.6 = (f32[2,3,64,256]{3,2,1,0:T(8,128)S(1)}, f32[2,3,64,256]{3,2,1,0:T(8,128)S(1)}, u32[]{:S(2)}, u32[]{:S(2)}) collective-permute-start(f32[2,3,64,256]{3,2,1,0:T(8,128)S(1)} %get-tuple-element.9), channel_id=1, source_target_pairs={{4,0},{8,4},{12,8},{16,12},{20,16},{24,20},{28,24},{32,28},{36,32}... | collective-permute-start | bytes 1179656 | tf_op jit(solution)/shard_map/ppermute | solution.py:23
  158.1 10.5 %collective-permute-start.7 = (f32[2,3,64,256]{3,2,1,0:T(8,128)S(1)}, f32[2,3,64,256]{3,2,1,0:T(8,128)S(1)}, u32[]{:S(2)}, u32[]{:S(2)}) collective-permute-start(f32[2,3,64,256]{3,2,1,0:T(8,128)S(1)} %get-tuple-element.8), channel_id=1, source_target_pairs={{252,0},{0,4},{4,8},{8,12},{12,16},{16,20},{20,24},{24,28},{28,32}... | collective-permute-start | bytes 1179656 | tf_op jit(solution)/shard_map/ppermute | solution.py:23
  (1 other events, 1.0 us)
Sparse Core Ops, SparseCore 0:
  83.5 31.3 reduce-scatter.4
  117.5 34.1 reduce-scatter.2

commit v3 on v2

--- a/solution.py
+++ b/solution.py
@@ -71,6 +71,28 @@
     )
 
 
+def ring_scatter(full):
+    count = lax.axis_size("mat")
+    me = lax.axis_index("mat")
+    share = full.shape[1] // count
+    split = full.shape[-1] // 2
+    halves = (full[..., :split], full[..., split:])
+    forward = [(i, (i + 1) % count) for i in range(count)]
+    backward = [((i + 1) % count, i) for i in range(count)]
+
+    def chunk(values, index):
+        return lax.dynamic_slice_in_dim(values, index * share, share, axis=1)
+
+    ahead = chunk(halves[0], lax.rem(me + count - 1, count))
+    behind = chunk(halves[1], lax.rem(me + 1, count))
+    for step in range(count - 1):
+        ahead = lax.ppermute(ahead, "mat", forward)
+        behind = lax.ppermute(behind, "mat", backward)
+        ahead = ahead + chunk(halves[0], lax.rem(me + 2 * count - 2 - step, count))
+        behind = behind + chunk(halves[1], lax.rem(me + 2 + step, count))
+    return jnp.concatenate([ahead, behind], axis=-1)
+
+
 def on_device(orbitals, potential, centre_first, centre_second, centre_third, correlation_pairs):
     block_orbs, window_cells, second_cells, third_cells = orbitals.shape
     patch_cells = potential.shape[0]
@@ -141,8 +163,8 @@
             for a in range(3)
         ]
     )
-    gram_part = lax.psum_scatter(gram_full, "mat", scatter_dimension=1, tiled=True)
-    energy_part = lax.psum_scatter(energy_full, "mat", scatter_dimension=1, tiled=True)
+    gram_part = ring_scatter(gram_full)
+    energy_part = ring_scatter(energy_full)
     col_count = block_orbs // mat_count
     strips = jnp.stack([gram_part, energy_part])
     assembled = jnp.pad(strips[:, :, :, 1], ((0, 0), (1, 1), (0, 0), (0, 0)))

time: 178 us -> 146 us (0.82)
  waiting for transfers between devices: 89.7 us -> 45.5 us
  starting transfers between devices: 20.2 us -> 41 us
  between operations: 14.5 us -> 1.24 us
  local copies, waits for them, and re-layouts: 7.84 us -> 11.9 us
    reduce_scatter x2 -> x0, waiting for transfers between devices: 55.9 us -> none  [the longest x1 36.7 us: on_device(): lax.psum_scatter(gram_full, 'mat', scatter_dimension=1, tiled=True)]
    ppermute x0 -> x12, starting transfers between devices: none -> 20.2 us  [the longest x6 19 us: ring_scatter(): ahead = lax.ppermute(ahead, 'mat', forward)]
    ppermute x0 -> x12, waiting for transfers between devices: none -> 16.4 us  [the longest x6 9.13 us: ring_scatter(): ahead = lax.ppermute(ahead, 'mat', forward)]
    ppermute x1, waiting for transfers between devices: 8.68 us -> 3.69 us  [on_device(): row_above = lax.ppermute(masked[:, :, second_cells - 1], 'mat', up)]
    convert_element_type x3, other arithmetic: 2.05 us -> 5.85 us  [stencil(): centre_cells = extended[:, 1:-1, 1:-1, :].astype(jnp.float32)]
    ppermute x1, waiting for transfers between devices: 5.14 us -> 7.66 us  [on_device(): row_below = lax.ppermute(masked[:, :, 0], 'mat', down)]
    ppermute x6, waiting for transfers between devices: 19.9 us -> 17.8 us  [passed_along(): return lax.ppermute(block, axis, route)]
  transfers between devices with their start and end apart: 10 -> 20, of which waited for: 8 -> 12; matrix products, arithmetic and copies ran while one was open for 16% -> 18% of each run, Pallas kernels for 0% -> 0%
where the time goes in v3:
time: 146 us; the launch traced here: 145 us
  waiting for transfers between devices  45.5 us (31%)
  starting transfers between devices  41 us (28%)
  other arithmetic  26.4 us (18%)
  matrix products  19.2 us (13%)
  local copies, waits for them, and re-layouts  11.9 us (8%)
    ppermute x6, starting transfers between devices, ring_scatter(): ahead = lax.ppermute(ahead, 'mat', forward)  19 us
    ppermute x6, starting transfers between devices, passed_along(): return lax.ppermute(block, axis, route)  18.5 us
    dot_general x18, matrix products, pair_product(): lax.dot_general(left, right, (((1, 2, 3), (1, 2, 3)), ((), ())), preferre...  17.9 us
    ppermute x6, waiting for transfers between devices, passed_along(): return lax.ppermute(block, axis, route)  17.8 us
    convert_element_type x2, other arithmetic, on_device(): stencil(ext, potential).astype(jnp.bfloat16)  10.7 us
    ppermute x6, waiting for transfers between devices, ring_scatter(): ahead = lax.ppermute(ahead, 'mat', forward)  9.13 us
    ppermute x1, waiting for transfers between devices, on_device(): row_below = lax.ppermute(masked[:, :, 0], 'mat', down)  7.66 us
    ppermute x6, waiting for transfers between devices, ring_scatter(): behind = lax.ppermute(behind, 'mat', backward)  7.22 us
  transfers between devices with their start and end apart: 20, of which 12 were waited for; matrix products, arithmetic and copies ran while one was open for 18% of the time, Pallas kernels for 0%

profile of v3, /device:TPU:6, one launch (start us, length us, event | category | flops | bytes accessed | tf_op | source)
XLA Modules:
  0.0 145.2 jit_solution(8881132000672934051)
XLA Ops:
  2.9 5.9 %fusion.1 = bf16[256,12,8,128]{3,0,2,1:T(8,128)(2,1)S(1)} fusion(bf16[256,12,8,128]{3,2,1,0:T(8,128)(2,1)} %param.6, s32[256,128]{1,0:T(8,128)S(1)} %subtract_multiply_fusion, s32[256,12,8]{0,2,1:T(8,128)S(1)} %broadcast_add_fusion, pred[12]{0:T(512)(128)(4,1)S(1)} %compare_and_fusion), kind=kLoop, calls=%fused_computation.2 | loop fusion | flops 12582912 | bytes 12812300 | tf_op jit(solution)/shard_map/jit(_where)/select_n | solution.py:114
  10.3 2.2 %collective-permute-start.8 = (bf16[256,12,128]{2,0,1:T(8,128)(2,1)}, bf16[256,12,128]{2,0,1:T(8,128)(2,1)S(1)}, u32[]{:S(2)}, u32[]{:S(2)}) collective-permute-start(bf16[256,12,128]{2,0,1:T(8,128)(2,1)} %get-tuple-element.5), channel_id=1, source_target_pairs={{0,1},{1,2},{2,3},{3,0},{4,5},{5,6},{6,7},{7,4},{8,9},{9,10},{10,1... | collective-permute-start | bytes 2359304 | tf_op jit(solution)/shard_map/ppermute | solution.py:123
  12.6 3.6 %slice_convert_fusion.2 = (f32[256,4,8,128]{3,0,2,1:T(8,128)}, bf16[256,4,8,128]{3,0,2,1:T(8,128)(2,1)}, bf16[256,4,8,128]{3,0,2,1:T(8,128)(2,1)}) fusion(bf16[256,12,8,128]{3,0,2,1:T(8,128)(2,1)S(1)} %fusion.1), kind=kLoop, calls=%fused_computation.97 | loop fusion | flops 1048576 | bytes 14680064 | tf_op jit(solution)/shard_map/convert_element_type | solution.py:54
  16.2 7.0 %collective-permute-start.1 = (bf16[256,4,8,128]{3,0,2,1:T(8,128)(2,1)}, bf16[256,4,8,128]{3,0,2,1:T(8,128)(2,1)}, u32[]{:S(2)}, u32[]{:S(2)}) collective-permute-start(bf16[256,4,8,128]{3,0,2,1:T(8,128)(2,1)} %get-tuple-element.3), channel_id=1, source_target_pairs={{4,0},{8,4},{12,8},{16,12},{20,16},{24,20},{28,24},{32,28},{36,32}... | collective-permute-start | bytes 6291464 | tf_op jit(solution)/shard_map/ppermute | solution.py:23
  23.2 3.0 %convolution_bitcast_fusion.1 = f32[256,1,256]{2,0,1:T(8,128)S(1)} fusion(bf16[256,12,8,128]{3,0,2,1:T(8,128)(2,1)} %copy-done), kind=kOutput, calls=%fused_computation.66 | convolution fusion | flops 536870912 | bytes 8650752 | tf_op jit(solution)/shard_map/dot_general | solution.py:69
  26.1 3.7 %collective-permute-done.8 = bf16[256,12,128]{2,0,1:T(8,128)(2,1)S(1)} collective-permute-done((bf16[256,12,128]{2,0,1:T(8,128)(2,1)}, bf16[256,12,128]{2,0,1:T(8,128)(2,1)S(1)}, u32[]{:S(2)}, u32[]{:S(2)}) %collective-permute-start.8) | collective-permute-done | bytes 786464 | tf_op jit(solution)/shard_map/ppermute | solution.py:123
  29.9 7.7 %collective-permute-done.9 = bf16[256,12,128]{2,0,1:T(8,128)(2,1)} collective-permute-done((bf16[256,12,128]{2,0,1:T(8,128)(2,1)}, bf16[256,12,128]{2,0,1:T(8,128)(2,1)}, u32[]{:S(2)}, u32[]{:S(2)}) %collective-permute-start.9) | collective-permute-done | bytes 786464 | tf_op jit(solution)/shard_map/ppermute | solution.py:124
  38.8 5.1 %collective-permute-start.11 = (bf16[2,256,4,128]{3,1,2,0:T(8,128)(2,1)S(1)}, bf16[2,256,4,128]{3,1,2,0:T(8,128)(2,1)S(1)}, u32[]{:S(2)}, u32[]{:S(2)}) collective-permute-start(bf16[2,256,4,128]{3,1,2,0:T(8,128)(2,1)S(1)} %pad_maximum_fusion.9), channel_id=1, source_target_pairs={{4,0},{8,4},{12,8},{16,12},{20,16},{24,20},{28,24},{32,28},{36,32}... | collective-permute-start | bytes 1572872 | tf_op jit(solution)/shard_map/ppermute | solution.py:23
  45.0 6.8 %collective-permute-done.10 = bf16[2,256,4,128]{3,1,2,0:T(8,128)(2,1)S(1)} collective-permute-done((bf16[2,256,4,128]{3,1,2,0:T(8,128)(2,1)S(1)}, bf16[2,256,4,128]{3,1,2,0:T(8,128)(2,1)S(1)}, u32[]{:S(2)}, u32[]{:S(2)}) %collective-permute-start.10) | collective-permute-done | bytes 524320 | tf_op jit(solution)/shard_map/ppermute | solution.py:23
  57.0 6.1 %fusion.7 = (bf16[256,4,8,128]{3,0,2,1:T(8,128)(2,1)S(1)}, bf16[256,4,8,128]{3,0,2,1:T(8,128)(2,1)S(1)}) fusion(f32[256,4,8,128]{3,0,2,1:T(8,128)S(1)} %slice_convert_fusion.1, bf16[256,4,8,128]{3,0,2,1:T(8,128)(2,1)S(1)} %collective-permute-done, bf16[256,6,8,128]{3,0,2,1:T(8,128)(2,1)S(1)} %concatenate.48, ...), kind=kLoop, calls=%fused_computation.14 | loop fusion | flops 35651584 | bytes 28852224 | tf_op jit(solution)/shard_map/convert_element_type | solution.py:155
  73.0 4.5 %fusion.19 = bf16[256,4,8,128]{3,0,2,1:T(8,128)(2,1)S(1)} fusion(f32[256,4,8,128]{3,0,2,1:T(8,128)S(1)} %slice_convert_fusion, bf16[256,4,8,128]{3,0,2,1:T(8,128)(2,1)} %collective-permute-done.1, bf16[256,6,8,128]{3,0,2,1:T(8,128)(2,1)S(1)} %concatenate.54, bf16[256,6,1,128]{3,0,2,1:T(8,128)(2,1)S(1)} %get-tuple-element.23, ...), kind=kLoop, calls=%fused_computation.26 | loop fusion | flops 17825792 | bytes 14434304 | tf_op jit(solution)/shard_map/convert_element_type | solution.py:155
  92.2 2.8 %collective-permute-start.2 = (f32[3,64,3,128]{3,1,2,0:T(8,128)S(1)}, f32[3,64,3,128]{3,1,2,0:T(8,128)S(1)}, u32[]{:S(2)}, u32[]{:S(2)}) collective-permute-start(f32[3,64,3,128]{3,1,2,0:T(8,128)S(1)} %constant_dynamic-slice_fusion.3), channel_id=1, source_target_pairs={{0,1},{1,2},{2,3},{3,0},{4,5},{5,6},{6,7},{7,4},{8,9},{9,10},{10,1... | collective-permute-start | bytes 884744 | tf_op jit(solution)/shard_map/ppermute | solution.py:89
  95.1 3.3 %collective-permute-start.13 = (f32[3,64,3,128]{3,1,2,0:T(8,128)S(1)}, f32[3,64,3,128]{3,1,2,0:T(8,128)S(1)}, u32[]{:S(2)}, u32[]{:S(2)}) collective-permute-start(f32[3,64,3,128]{3,1,2,0:T(8,128)S(1)} %dynamic-slice_add_fusion.5), channel_id=1, source_target_pairs={{0,1},{1,2},{2,3},{3,0},{4,5},{5,6},{6,7},{7,4},{8,9},{9,10},{10,1... | collective-permute-start | bytes 884744 | tf_op jit(solution)/shard_map/ppermute | solution.py:89
  98.6 3.9 %collective-permute-done.2 = f32[3,64,3,128]{3,1,2,0:T(8,128)S(1)} collective-permute-done((f32[3,64,3,128]{3,1,2,0:T(8,128)S(1)}, f32[3,64,3,128]{3,1,2,0:T(8,128)S(1)}, u32[]{:S(2)}, u32[]{:S(2)}) %collective-permute-start.2) | collective-permute-done | bytes 294944 | tf_op jit(solution)/shard_map/ppermute | solution.py:89
  102.5 3.8 %collective-permute-start.3 = (f32[3,64,3,128]{3,1,2,0:T(8,128)S(1)}, f32[3,64,3,128]{3,1,2,0:T(8,128)S(1)}, u32[]{:S(2)}, u32[]{:S(2)}) collective-permute-start(f32[3,64,3,128]{3,1,2,0:T(8,128)S(1)} %dynamic-slice_add_fusion.11), channel_id=1, source_target_pairs={{0,1},{1,2},{2,3},{3,0},{4,5},{5,6},{6,7},{7,4},{8,9},{9,10},{10,1... | collective-permute-start | bytes 884744 | tf_op jit(solution)/shard_map/ppermute | solution.py:89
  106.4 2.4 %collective-permute-done.13 = f32[3,64,3,128]{3,1,2,0:T(8,128)S(1)} collective-permute-done((f32[3,64,3,128]{3,1,2,0:T(8,128)S(1)}, f32[3,64,3,128]{3,1,2,0:T(8,128)S(1)}, u32[]{:S(2)}, u32[]{:S(2)}) %collective-permute-start.13) | collective-permute-done | bytes 294944 | tf_op jit(solution)/shard_map/ppermute | solution.py:89
  108.8 3.8 %collective-permute-start.14 = (f32[3,64,3,128]{3,1,2,0:T(8,128)S(1)}, f32[3,64,3,128]{3,1,2,0:T(8,128)S(1)}, u32[]{:S(2)}, u32[]{:S(2)}) collective-permute-start(f32[3,64,3,128]{3,1,2,0:T(8,128)S(1)} %dynamic-slice_add_fusion.4), channel_id=1, source_target_pairs={{0,1},{1,2},{2,3},{3,0},{4,5},{5,6},{6,7},{7,4},{8,9},{9,10},{10,1... | collective-permute-start | bytes 884744 | tf_op jit(solution)/shard_map/ppermute | solution.py:89
  112.7 2.4 %collective-permute-done.3 = f32[3,64,3,128]{3,1,2,0:T(8,128)S(1)} collective-permute-done((f32[3,64,3,128]{3,1,2,0:T(8,128)S(1)}, f32[3,64,3,128]{3,1,2,0:T(8,128)S(1)}, u32[]{:S(2)}, u32[]{:S(2)}) %collective-permute-start.3) | collective-permute-done | bytes 294944 | tf_op jit(solution)/shard_map/ppermute | solution.py:89
  115.1 3.8 %collective-permute-start.4 = (f32[3,64,3,128]{3,1,2,0:T(8,128)S(1)}, f32[3,64,3,128]{3,1,2,0:T(8,128)S(1)}, u32[]{:S(2)}, u32[]{:S(2)}) collective-permute-start(f32[3,64,3,128]{3,1,2,0:T(8,128)S(1)} %dynamic-slice_add_fusion.10), channel_id=1, source_target_pairs={{0,1},{1,2},{2,3},{3,0},{4,5},{5,6},{6,7},{7,4},{8,9},{9,10},{10,1... | collective-permute-start | bytes 884744 | tf_op jit(solution)/shard_map/ppermute | solution.py:89
  119.6 3.5 %collective-permute-done.17 = f32[3,64,3,128]{3,1,2,0:T(8,128)S(1)} collective-permute-done((f32[3,64,3,128]{3,1,2,0:T(8,128)S(1)}, f32[3,64,3,128]{3,1,2,0:T(8,128)S(1)}, u32[]{:S(2)}, u32[]{:S(2)}) %collective-permute-start.17) | collective-permute-done | bytes 294944 | tf_op jit(solution)/shard_map/ppermute | solution.py:90
  123.2 3.7 %collective-permute-done.7 = f32[3,64,3,128]{3,1,2,0:T(8,128)S(1)} collective-permute-done((f32[3,64,3,128]{3,1,2,0:T(8,128)S(1)}, f32[3,64,3,128]{3,1,2,0:T(8,128)S(1)}, u32[]{:S(2)}, u32[]{:S(2)}) %collective-permute-start.7) | collective-permute-done | bytes 294944 | tf_op jit(solution)/shard_map/ppermute | solution.py:90
  127.1 6.3 %collective-permute-start.18 = (f32[2,3,64,256]{3,2,1,0:T(8,128)S(1)}, f32[2,3,64,256]{3,2,1,0:T(8,128)S(1)}, u32[]{:S(2)}, u32[]{:S(2)}) collective-permute-start(f32[2,3,64,256]{3,2,1,0:T(8,128)S(1)} %get-tuple-element.13), channel_id=1, source_target_pairs={{4,0},{8,4},{12,8},{16,12},{20,16},{24,20},{28,24},{32,28},{36,32}... | collective-permute-start | bytes 1179656 | tf_op jit(solution)/shard_map/ppermute | solution.py:23
  133.7 5.1 %collective-permute-done.18 = f32[2,3,64,256]{3,2,1,0:T(8,128)S(1)} collective-permute-done((f32[2,3,64,256]{3,2,1,0:T(8,128)S(1)}, f32[2,3,64,256]{3,2,1,0:T(8,128)S(1)}, u32[]{:S(2)}, u32[]{:S(2)}) %collective-permute-start.18) | collective-permute-done | bytes 393248 | tf_op jit(solution)/shard_map/ppermute | solution.py:23
  138.8 5.2 %collective-permute-done.19 = f32[2,3,64,256]{3,2,1,0:T(8,128)S(1)} collective-permute-done((f32[2,3,64,256]{3,2,1,0:T(8,128)S(1)}, f32[2,3,64,256]{3,2,1,0:T(8,128)S(1)}, u32[]{:S(2)}, u32[]{:S(2)}) %collective-permute-start.19) | collective-permute-done | bytes 393248 | tf_op jit(solution)/shard_map/ppermute | solution.py:23
  (107 shorter events, 38.4 us)
Async XLA Ops:
  8.9 14.3 %copy-start = (bf16[256,12,8,128]{3,0,2,1:T(8,128)(2,1)}, bf16[256,12,8,128]{3,0,2,1:T(8,128)(2,1)S(1)}, u32[]{:S(2)}) copy-start(bf16[256,12,8,128]{3,0,2,1:T(8,128)(2,1)S(1)} %fusion.1) | copy-start | bytes 18874372
  10.3 19.5 %collective-permute-start.8 = (bf16[256,12,128]{2,0,1:T(8,128)(2,1)}, bf16[256,12,128]{2,0,1:T(8,128)(2,1)S(1)}, u32[]{:S(2)}, u32[]{:S(2)}) collective-permute-start(bf16[256,12,128]{2,0,1:T(8,128)(2,1)} %get-tuple-element.5), channel_id=1, source_target_pairs={{0,1},{1,2},{2,3},{3,0},{4,5},{5,6},{6,7},{7,4},{8,9},{9,10},{10,1... | collective-permute-start | bytes 2359304 | tf_op jit(solution)/shard_map/ppermute | solution.py:123
  16.2 36.5 %collective-permute-start = (bf16[256,4,8,128]{3,0,2,1:T(8,128)(2,1)}, bf16[256,4,8,128]{3,0,2,1:T(8,128)(2,1)S(1)}, u32[]{:S(2)}, u32[]{:S(2)}) collective-permute-start(bf16[256,4,8,128]{3,0,2,1:T(8,128)(2,1)} %get-tuple-element.4), channel_id=1, source_target_pairs={{252,0},{0,4},{4,8},{8,12},{12,16},{16,20},{20,24},{24,28},{28,32}... | collective-permute-start | bytes 6291464 | tf_op jit(solution)/shard_map/ppermute | solution.py:23
  16.2 21.4 %collective-permute-start.9 = (bf16[256,12,128]{2,0,1:T(8,128)(2,1)}, bf16[256,12,128]{2,0,1:T(8,128)(2,1)}, u32[]{:S(2)}, u32[]{:S(2)}) collective-permute-start(bf16[256,12,128]{2,0,1:T(8,128)(2,1)} %get-tuple-element.6), channel_id=1, source_target_pairs={{1,0},{2,1},{3,2},{0,3},{5,4},{6,5},{7,6},{4,7},{9,8},{10,9},{11,1... | collective-permute-start | bytes 2359304 | tf_op jit(solution)/shard_map/ppermute | solution.py:124
  16.2 49.9 %collective-permute-start.1 = (bf16[256,4,8,128]{3,0,2,1:T(8,128)(2,1)}, bf16[256,4,8,128]{3,0,2,1:T(8,128)(2,1)}, u32[]{:S(2)}, u32[]{:S(2)}) collective-permute-start(bf16[256,4,8,128]{3,0,2,1:T(8,128)(2,1)} %get-tuple-element.3), channel_id=1, source_target_pairs={{4,0},{8,4},{12,8},{16,12},{20,16},{24,20},{28,24},{32,28},{36,32}... | collective-permute-start | bytes 6291464 | tf_op jit(solution)/shard_map/ppermute | solution.py:23
  38.7 13.2 %collective-permute-start.10 = (bf16[2,256,4,128]{3,1,2,0:T(8,128)(2,1)S(1)}, bf16[2,256,4,128]{3,1,2,0:T(8,128)(2,1)S(1)}, u32[]{:S(2)}, u32[]{:S(2)}) collective-permute-start(bf16[2,256,4,128]{3,1,2,0:T(8,128)(2,1)S(1)} %pad_maximum_fusion.8), channel_id=1, source_target_pairs={{252,0},{0,4},{4,8},{8,12},{12,16},{16,20},{20,24},{24,28},{28,32}... | collective-permute-start | bytes 1572872 | tf_op jit(solution)/shard_map/ppermute | solution.py:23
  38.8 13.7 %collective-permute-start.11 = (bf16[2,256,4,128]{3,1,2,0:T(8,128)(2,1)S(1)}, bf16[2,256,4,128]{3,1,2,0:T(8,128)(2,1)S(1)}, u32[]{:S(2)}, u32[]{:S(2)}) collective-permute-start(bf16[2,256,4,128]{3,1,2,0:T(8,128)(2,1)S(1)} %pad_maximum_fusion.9), channel_id=1, source_target_pairs={{4,0},{8,4},{12,8},{16,12},{20,16},{24,20},{28,24},{32,28},{36,32}... | collective-permute-start | bytes 1572872 | tf_op jit(solution)/shard_map/ppermute | solution.py:23
  53.2 3.8 %slice-start.2 = ((bf16[256,12,8,128]{3,0,2,1:T(8,128)(2,1)}), bf16[256,6,8,128]{3,0,2,1:T(8,128)(2,1)S(1)}, s32[]{:S(2)}) async-start(bf16[256,12,8,128]{3,0,2,1:T(8,128)(2,1)} %copy-done), calls=%async_computation.2 | async-start | bytes 6291456 | tf_op jit(solution)/shard_map/slice | solution.py:138
  53.2 3.8 %copy-start.2 = (f32[4,8,128]{2,1,0:T(8,128)S(1)}, f32[4,8,128]{2,1,0:T(8,128)}, u32[]{:S(2)}) copy-start(f32[4,8,128]{2,1,0:T(8,128)} %param.7) | copy-start | bytes 49156
  83.2 11.9 %collective-permute-start.12 = (f32[3,64,3,128]{3,1,2,0:T(8,128)S(1)}, f32[3,64,3,128]{3,1,2,0:T(8,128)S(1)}, u32[]{:S(2)}, u32[]{:S(2)}) collective-permute-start(f32[3,64,3,128]{3,1,2,0:T(8,128)S(1)} %constant_dynamic-slice_fusion.1), channel_id=1, source_target_pairs={{0,1},{1,2},{2,3},{3,0},{4,5},{5,6},{6,7},{7,4},{8,9},{9,10},{10,1... | collective-permute-start | bytes 884744 | tf_op jit(solution)/shard_map/ppermute | solution.py:89
  84.8 13.6 %collective-permute-start.15 = (f32[3,64,3,128]{3,1,2,0:T(8,128)S(1)}, f32[3,64,3,128]{3,1,2,0:T(8,128)S(1)}, u32[]{:S(2)}, u32[]{:S(2)}) collective-permute-start(f32[3,64,3,128]{3,1,2,0:T(8,128)S(1)} %constant_dynamic-slice_fusion), channel_id=1, source_target_pairs={{1,0},{2,1},{3,2},{0,3},{5,4},{6,5},{7,6},{4,7},{9,8},{10,9},{11,1... | collective-permute-start | bytes 884744 | tf_op jit(solution)/shard_map/ppermute | solution.py:90
  92.2 10.3 %collective-permute-start.2 = (f32[3,64,3,128]{3,1,2,0:T(8,128)S(1)}, f32[3,64,3,128]{3,1,2,0:T(8,128)S(1)}, u32[]{:S(2)}, u32[]{:S(2)}) collective-permute-start(f32[3,64,3,128]{3,1,2,0:T(8,128)S(1)} %constant_dynamic-slice_fusion.3), channel_id=1, source_target_pairs={{0,1},{1,2},{2,3},{3,0},{4,5},{5,6},{6,7},{7,4},{8,9},{9,10},{10,1... | collective-permute-start | bytes 884744 | tf_op jit(solution)/shard_map/ppermute | solution.py:89
  95.0 11.3 %collective-permute-start.5 = (f32[3,64,3,128]{3,1,2,0:T(8,128)S(1)}, f32[3,64,3,128]{3,1,2,0:T(8,128)S(1)}, u32[]{:S(2)}, u32[]{:S(2)}) collective-permute-start(f32[3,64,3,128]{3,1,2,0:T(8,128)S(1)} %constant_dynamic-slice_fusion.2), channel_id=1, source_target_pairs={{1,0},{2,1},{3,2},{0,3},{5,4},{6,5},{7,6},{4,7},{9,8},{10,9},{11,1... | collective-permute-start | bytes 884744 | tf_op jit(solution)/shard_map/ppermute | solution.py:90
  95.1 13.6 %collective-permute-start.13 = (f32[3,64,3,128]{3,1,2,0:T(8,128)S(1)}, f32[3,64,3,128]{3,1,2,0:T(8,128)S(1)}, u32[]{:S(2)}, u32[]{:S(2)}) collective-permute-start(f32[3,64,3,128]{3,1,2,0:T(8,128)S(1)} %dynamic-slice_add_fusion.5), channel_id=1, source_target_pairs={{0,1},{1,2},{2,3},{3,0},{4,5},{5,6},{6,7},{7,4},{8,9},{9,10},{10,1... | collective-permute-start | bytes 884744 | tf_op jit(solution)/shard_map/ppermute | solution.py:89
  98.5 14.1 %collective-permute-start.16 = (f32[3,64,3,128]{3,1,2,0:T(8,128)S(1)}, f32[3,64,3,128]{3,1,2,0:T(8,128)S(1)}, u32[]{:S(2)}, u32[]{:S(2)}) collective-permute-start(f32[3,64,3,128]{3,1,2,0:T(8,128)S(1)} %dynamic-slice_add_fusion.2), channel_id=1, source_target_pairs={{1,0},{2,1},{3,2},{0,3},{5,4},{6,5},{7,6},{4,7},{9,8},{10,9},{11,1... | collective-permute-start | bytes 884744 | tf_op jit(solution)/shard_map/ppermute | solution.py:90
  102.5 12.6 %collective-permute-start.3 = (f32[3,64,3,128]{3,1,2,0:T(8,128)S(1)}, f32[3,64,3,128]{3,1,2,0:T(8,128)S(1)}, u32[]{:S(2)}, u32[]{:S(2)}) collective-permute-start(f32[3,64,3,128]{3,1,2,0:T(8,128)S(1)} %dynamic-slice_add_fusion.11), channel_id=1, source_target_pairs={{0,1},{1,2},{2,3},{3,0},{4,5},{5,6},{6,7},{7,4},{8,9},{9,10},{10,1... | collective-permute-start | bytes 884744 | tf_op jit(solution)/shard_map/ppermute | solution.py:89
  106.3 12.6 %collective-permute-start.6 = (f32[3,64,3,128]{3,1,2,0:T(8,128)S(1)}, f32[3,64,3,128]{3,1,2,0:T(8,128)S(1)}, u32[]{:S(2)}, u32[]{:S(2)}) collective-permute-start(f32[3,64,3,128]{3,1,2,0:T(8,128)S(1)} %dynamic-slice_add_fusion.8), channel_id=1, source_target_pairs={{1,0},{2,1},{3,2},{0,3},{5,4},{6,5},{7,6},{4,7},{9,8},{10,9},{11,1... | collective-permute-start | bytes 884744 | tf_op jit(solution)/shard_map/ppermute | solution.py:90
  108.8 10.7 %collective-permute-start.14 = (f32[3,64,3,128]{3,1,2,0:T(8,128)S(1)}, f32[3,64,3,128]{3,1,2,0:T(8,128)S(1)}, u32[]{:S(2)}, u32[]{:S(2)}) collective-permute-start(f32[3,64,3,128]{3,1,2,0:T(8,128)S(1)} %dynamic-slice_add_fusion.4), channel_id=1, source_target_pairs={{0,1},{1,2},{2,3},{3,0},{4,5},{5,6},{6,7},{7,4},{8,9},{9,10},{10,1... | collective-permute-start | bytes 884744 | tf_op jit(solution)/shard_map/ppermute | solution.py:89
  112.6 10.4 %collective-permute-start.17 = (f32[3,64,3,128]{3,1,2,0:T(8,128)S(1)}, f32[3,64,3,128]{3,1,2,0:T(8,128)S(1)}, u32[]{:S(2)}, u32[]{:S(2)}) collective-permute-start(f32[3,64,3,128]{3,1,2,0:T(8,128)S(1)} %dynamic-slice_add_fusion.1), channel_id=1, source_target_pairs={{1,0},{2,1},{3,2},{0,3},{5,4},{6,5},{7,6},{4,7},{9,8},{10,9},{11,1... | collective-permute-start | bytes 884744 | tf_op jit(solution)/shard_map/ppermute | solution.py:90
  115.1 8.0 %collective-permute-start.4 = (f32[3,64,3,128]{3,1,2,0:T(8,128)S(1)}, f32[3,64,3,128]{3,1,2,0:T(8,128)S(1)}, u32[]{:S(2)}, u32[]{:S(2)}) collective-permute-start(f32[3,64,3,128]{3,1,2,0:T(8,128)S(1)} %dynamic-slice_add_fusion.10), channel_id=1, source_target_pairs={{0,1},{1,2},{2,3},{3,0},{4,5},{5,6},{6,7},{7,4},{8,9},{9,10},{10,1... | collective-permute-start | bytes 884744 | tf_op jit(solution)/shard_map/ppermute | solution.py:89
  118.9 8.0 %collective-permute-start.7 = (f32[3,64,3,128]{3,1,2,0:T(8,128)S(1)}, f32[3,64,3,128]{3,1,2,0:T(8,128)S(1)}, u32[]{:S(2)}, u32[]{:S(2)}) collective-permute-start(f32[3,64,3,128]{3,1,2,0:T(8,128)S(1)} %dynamic-slice_add_fusion.7), channel_id=1, source_target_pairs={{1,0},{2,1},{3,2},{0,3},{5,4},{6,5},{7,6},{4,7},{9,8},{10,9},{11,1... | collective-permute-start | bytes 884744 | tf_op jit(solution)/shard_map/ppermute | solution.py:90
  123.2 10.3 %copy-start.3 = (s32[2,5,2]{1,2,0:T(2,128)S(1)}, s32[2,5,2]{1,2,0:T(2,128)}, u32[]{:S(2)}) copy-start(s32[2,5,2]{1,2,0:T(2,128)} %param.11) | copy-start | bytes 244
  127.1 11.6 %collective-permute-start.18 = (f32[2,3,64,256]{3,2,1,0:T(8,128)S(1)}, f32[2,3,64,256]{3,2,1,0:T(8,128)S(1)}, u32[]{:S(2)}, u32[]{:S(2)}) collective-permute-start(f32[2,3,64,256]{3,2,1,0:T(8,128)S(1)} %get-tuple-element.13), channel_id=1, source_target_pairs={{4,0},{8,4},{12,8},{16,12},{20,16},{24,20},{28,24},{32,28},{36,32}... | collective-permute-start | bytes 1179656 | tf_op jit(solution)/shard_map/ppermute | solution.py:23
  133.5 10.5 %collective-permute-start.19 = (f32[2,3,64,256]{3,2,1,0:T(8,128)S(1)}, f32[2,3,64,256]{3,2,1,0:T(8,128)S(1)}, u32[]{:S(2)}, u32[]{:S(2)}) collective-permute-start(f32[2,3,64,256]{3,2,1,0:T(8,128)S(1)} %get-tuple-element.12), channel_id=1, source_target_pairs={{252,0},{0,4},{4,8},{8,12},{12,16},{16,20},{20,24},{24,28},{28,32}... | collective-permute-start | bytes 1179656 | tf_op jit(solution)/shard_map/ppermute | solution.py:23
  (3 other events, 7.5 us)
